TPU v7x, 512 devices: a whole 4x4x16 slice. The times are simulated.
512 devices in a mesh: dap: 128 (over x_hi, y, z), grp: 4 (over x_lo, core).
Axes of the slice: x: 4 (x_hi: 2, x_lo: 2; x = x_hi * 2 + x_lo), y: 4, z: 16, core: 2. Of those that a mesh axis runs over, the one named last changes fastest.
Arguments:
- pair_rep: bfloat16 [1024, 1024, 128], P('dap', 'grp'), may hold values from -6 to 6
- chain_ids: int32 [1024], replicated, may hold values from 0 to 7, never falling along the last dimension, each value on 1 to 256 neighbouring positions
- crop_lengths: int32 [8], replicated, may hold values from 64 to 256
- ln_in_gain: float32 [2, 128], replicated, may hold values from 0.1 to 1.9
- w_proj: bfloat16 [2, 128, 512], replicated, may hold values from -0.5 to 0.5
- w_gate: bfloat16 [2, 128, 128], replicated, may hold values from -0.5 to 0.5
- ln_out_gain: float32 [2, 128], replicated, may hold values from 0.1 to 1.9
- w_out: bfloat16 [2, 128, 128], replicated, may hold values from -0.5 to 0.5
Outputs:
- pair_out: bfloat16 [1024, 1024, 128], P('dap', 'grp')
Inputs may be any that keep to these rules, and one draw needn't show every extreme that they name: `chain_ids`: chain ids never fall along the residues; each chain holds 1 to 256 residues, and some chain exactly 256.
All inputs are finite; a program needn't handle non-finite values.
Results may differ from a plain program's by a relative error of at most 0.0095.
Values may be sent and summed in bfloat16 or wider, within the bound.
A program may use at most 64 MiB of HBM per device.

v0:
```python
import jax
import jax.numpy as jnp
from jax import lax
from jax.sharding import PartitionSpec as P

epsilon_norm = 1e-05


def residue_valid(chain_ids, crop_lengths):
    count = chain_ids.shape[0]
    chains = jnp.arange(crop_lengths.shape[0], dtype=jnp.int32)
    member = (chain_ids[:, None] == chains[None, :]).astype(jnp.int32)
    counts = jnp.sum(member, axis=0)
    starts = jnp.cumsum(counts) - counts
    first = jnp.sum(member * starts[None, :], axis=1)
    limit = jnp.sum(member * crop_lengths[None, :], axis=1)
    place = jnp.arange(count, dtype=jnp.int32) - first
    return (place < limit).astype(jnp.float32)


def layer_norm(values, gain, axis):
    centre = jnp.mean(values, axis=axis, keepdims=True)
    spread = jnp.mean((values - centre) ** 2, axis=axis, keepdims=True)
    return (values - centre) * lax.rsqrt(spread + epsilon_norm) * gain


def column_rows(right_chan):
    return lax.all_to_all(right_chan, "grp", split_axis=1, concat_axis=2, tiled=True)


def update(pair_tile, pair_mask, ln_in, w_proj, w_gate, ln_out, w_out, outgoing):
    hidden = w_out.shape[0]
    normed = layer_norm(pair_tile.astype(jnp.float32), ln_in, 2).astype(jnp.bfloat16)
    projected = jnp.einsum("rqc,cf->frq", normed, w_proj, preferred_element_type=jnp.float32)
    gate_value = jax.nn.sigmoid(
        jnp.einsum("rqc,cd->rqd", normed, w_gate, preferred_element_type=jnp.float32)
    )
    left_op = (
        jax.nn.sigmoid(projected[:hidden]) * projected[hidden : 2 * hidden] * pair_mask
    ).astype(jnp.bfloat16)
    right_op = (
        jax.nn.sigmoid(projected[2 * hidden : 3 * hidden]) * projected[3 * hidden :] * pair_mask
    ).astype(jnp.bfloat16)
    left_chan, right_chan = (
        lax.all_to_all(left_op, "dap", split_axis=0, concat_axis=1, tiled=True),
        lax.all_to_all(right_op, "dap", split_axis=0, concat_axis=1, tiled=True),
    )
    if outgoing:
        right_rows = column_rows(right_chan)
        triangle = jnp.einsum(
            "hik,hjk->hij",
            lax.all_gather(left_chan, "grp", axis=2, tiled=True),
            right_rows,
            preferred_element_type=jnp.float32,
        )
    else:
        triangle = jnp.einsum(
            "hki,hkj->hij",
            lax.all_gather(left_chan, "grp", axis=2, tiled=True),
            right_chan,
            preferred_element_type=jnp.float32,
        )
    returned = lax.all_to_all(
        triangle.astype(jnp.bfloat16), "dap", split_axis=1, concat_axis=0, tiled=True
    )
    normed_product = layer_norm(returned.astype(jnp.float32), ln_out[:, None, None], 0).astype(
        jnp.bfloat16
    )
    update_term = jnp.einsum(
        "hrq,hd->rqd", normed_product, w_out, preferred_element_type=jnp.float32
    )
    return (pair_tile.astype(jnp.float32) + gate_value * update_term).astype(jnp.bfloat16)


def shards(pair_rep, chain_ids, crop_lengths, ln_in_gain, w_proj, w_gate, ln_out_gain, w_out):
    row_count = pair_rep.shape[0]
    column_count = pair_rep.shape[1]
    kept = residue_valid(chain_ids, crop_lengths)
    row_start = lax.axis_index("dap") * row_count
    column_start = lax.axis_index("grp") * column_count
    kept_rows = lax.dynamic_slice_in_dim(kept, row_start, row_count, 0)
    kept_columns = lax.dynamic_slice_in_dim(kept, column_start, column_count, 0)
    pair_mask = kept_rows[:, None] * kept_columns[None, :]
    pair_tile = pair_rep
    for layer_index, outgoing in ((0, True), (1, False)):
        pair_tile = update(
            pair_tile,
            pair_mask,
            ln_in_gain[layer_index],
            w_proj[layer_index],
            w_gate[layer_index],
            ln_out_gain[layer_index],
            w_out[layer_index],
            outgoing,
        )
    return pair_tile


def solution(mesh):
    placed = (P("dap", "grp", None), P(), P(), P(), P(), P(), P(), P())
    return jax.shard_map(
        shards, mesh=mesh, in_specs=placed, out_specs=P("dap", "grp", None), check_vma=False
    )
```

profile of v0, /device:TPU:25, one launch (start us, length us, event | category | flops | bytes accessed | tf_op | source)
XLA Modules:
  0.0 323.5 jit_solution(10404429011913691627)
XLA Ops:
  6.5 0.9 convert_reduce_fusion.2
  7.4 0.2 reduce-window.8
  7.6 0.8 select_reduce_fusion.1
  8.4 0.1 dynamic_slice.6
  8.5 0.1 dynamic_slice.7
  8.5 1.2 copy.79
  9.8 0.1 convert_reduce_fusion.1
  9.9 0.2 fusion.37
  10.1 0.1 broadcast_multiply_fusion
  10.2 0.8 convolution_bitcast_fusion.1
  11.0 0.6 fusion.66
  11.6 0.4 copy.83
  12.0 51.9 %all_to_all.78 = bf16[128,8,256]{2,1,0:T(8,128)(2,1)} all-to-all(bf16[128,8,256]{2,1,0:T(8,128)(2,1)S(1)} %copy.83), channel_id=1, replica_groups=mesh['dap'=128,'grp'=4] {'dap'}, dimensions={0} | all-to-all | bytes 1048576 | tf_op jit(solution)/shard_map/all_to_all | solution.py:45
  63.9 0.0 all-gather.3.cloned.1.call-update
  63.9 0.4 copy.84
  64.3 41.1 %all_to_all.79 = bf16[128,8,256]{2,1,0:T(8,128)(2,1)S(1)} all-to-all(bf16[128,8,256]{2,1,0:T(8,128)(2,1)S(1)} %copy.84), channel_id=1, replica_groups=mesh['dap'=128,'grp'=4] {'dap'}, dimensions={0} | all-to-all | bytes 1048576 | tf_op jit(solution)/shard_map/all_to_all | solution.py:46
  105.5 0.8 copy.125
  106.3 0.5 broadcast.180
  106.8 3.8 %reduce = bf16[1024,256]{1,0:T(8,128)(2,1)S(1)} reduce(bf16[1024,1,256]{2,1,0:T(2,128)(2,1)S(1)} %bitcast.131, bf16[]{:T(256)} %broadcast.180), dimensions={1}, to_apply=%bitcast.123.reduce_sub_computation | reduce | bytes 1048578
  110.6 0.1 reshape.204
  110.7 14.7 %all_to_all.80 = bf16[4,2,32768]{2,1,0:T(2,128)(2,1)S(1)} all-to-all(bf16[4,2,32768]{2,1,0:T(2,128)(2,1)S(1)} %reshape.204), channel_id=1, replica_groups=mesh['dap'=128,'grp'=4] {'grp'}, dimensions={0} | all-to-all | bytes 1048576 | tf_op jit(solution)/shard_map/all_to_all | solution.py:28
  125.4 0.5 reshape.205
  125.9 0.1 copy.107
  126.0 0.2 copy.86
  126.2 0.0 all-gather.3.cloned.1.call-done
  126.2 2.3 fusion.31
  128.5 0.8 copy.124
  129.4 3.9 %reduce.1 = bf16[1024,256]{1,0:T(8,128)(2,1)S(1)} reduce(bf16[1024,1,256]{2,1,0:T(2,128)(2,1)S(1)} %bitcast.133, bf16[]{:T(256)} %broadcast.180), dimensions={1}, to_apply=%bitcast.122.reduce_sub_computation | reduce | bytes 1048578
  133.3 1.0 reshape.206
  134.3 8.0 %all-to-all-start.3 = ((bf16[128,2,1024]{2,1,0:T(2,128)(2,1)}), bf16[128,2,1024]{2,1,0:T(2,128)(2,1)S(1)}, u32[]{:S(2)}, u32[]{:S(2)}) async-start(bf16[128,2,1024]{2,1,0:T(2,128)(2,1)} %reshape.206), calls=%async_computation.3 | async-start | bytes 1048576 | tf_op jit(solution)/shard_map/all_to_all | solution.py:63
  142.3 0.0 all-gather.5.cloned.1.call-start
  142.3 0.1 mul.210
  142.4 0.1 mul.211
  142.5 30.1 %all-to-all-done.3 = bf16[128,2,1024]{2,1,0:T(2,128)(2,1)S(1)} async-done(((bf16[128,2,1024]{2,1,0:T(2,128)(2,1)}), bf16[128,2,1024]{2,1,0:T(2,128)(2,1)S(1)}, u32[]{:S(2)}, u32[]{:S(2)}) %all-to-all-start.3) | async-done | bytes 524320 | tf_op jit(solution)/shard_map/all_to_all | solution.py:63
  172.6 0.4 reshape.207
  173.0 0.1 fusion.15
  173.2 0.2 fusion.41
  173.4 0.2 fusion.75
  173.6 0.3 copy-done.1
  173.9 0.3 fusion.79
  174.2 0.6 convert_reduce_fusion
  174.8 0.2 fusion.34
  175.0 0.8 convolution_bitcast_fusion
  175.8 0.6 fusion.51
  176.4 0.4 copy.94
  176.8 41.6 %all_to_all.81 = bf16[128,8,256]{2,1,0:T(8,128)(2,1)} all-to-all(bf16[128,8,256]{2,1,0:T(8,128)(2,1)S(1)} %copy.94), channel_id=1, replica_groups=mesh['dap'=128,'grp'=4] {'dap'}, dimensions={0} | all-to-all | bytes 1048576 | tf_op jit(solution)/shard_map/all_to_all | solution.py:45
  218.4 0.0 all-gather.5.cloned.1.call-update
  218.4 0.4 copy.95
  218.8 41.5 %all_to_all.82 = bf16[128,8,256]{2,1,0:T(8,128)(2,1)S(1)} all-to-all(bf16[128,8,256]{2,1,0:T(8,128)(2,1)S(1)} %copy.95), channel_id=1, replica_groups=mesh['dap'=128,'grp'=4] {'dap'}, dimensions={0} | all-to-all | bytes 1048576 | tf_op jit(solution)/shard_map/all_to_all | solution.py:46
  260.3 2.4 fusion.28
  262.7 0.8 copy.123
  263.5 3.9 %reduce.2 = bf16[1024,256]{1,0:T(8,128)(2,1)S(1)} reduce(bf16[1024,1,256]{2,1,0:T(2,128)(2,1)S(1)} %bitcast.132, bf16[]{:T(256)} %broadcast.180), dimensions={1}, to_apply=%bitcast.121.reduce_sub_computation | reduce | bytes 1048578
  267.4 1.0 reshape.208
  268.4 13.1 %all-to-all-start.6 = ((bf16[128,2,1024]{2,1,0:T(2,128)(2,1)}), bf16[128,2,1024]{2,1,0:T(2,128)(2,1)S(1)}, u32[]{:S(2)}, u32[]{:S(2)}) async-start(bf16[128,2,1024]{2,1,0:T(2,128)(2,1)} %reshape.208), calls=%async_computation.6 | async-start | bytes 1048576 | tf_op jit(solution)/shard_map/all_to_all | solution.py:63
  281.6 0.1 mul.228
  281.6 0.1 mul.229
  281.7 32.0 %all-to-all-done.6 = bf16[128,2,1024]{2,1,0:T(2,128)(2,1)S(1)} async-done(((bf16[128,2,1024]{2,1,0:T(2,128)(2,1)}), bf16[128,2,1024]{2,1,0:T(2,128)(2,1)S(1)}, u32[]{:S(2)}, u32[]{:S(2)}) %all-to-all-start.6) | async-done | bytes 524320 | tf_op jit(solution)/shard_map/all_to_all | solution.py:63
  313.8 0.4 reshape.209
  314.2 0.1 fusion.13
  314.4 0.2 fusion.46
  314.6 0.2 fusion.74
  314.8 0.3 fusion.77
  315.1 0.6 fusion.17
  315.7 1.0 copy.100
  (23 shorter events, 0.1 us)
Async XLA Ops:
  6.5 3.5 %copy-start.2 = (f32[2,128]{1,0:T(2,128)S(1)}, f32[2,128]{1,0:T(2,128)}, u32[]{:S(2)}) copy-start(f32[2,128]{1,0:T(2,128)} %param.11) | copy-start | bytes 3076
  6.5 3.6 %copy-start = (bf16[2,128,512]{2,1,0:T(8,128)(2,1)S(1)}, bf16[2,128,512]{2,1,0:T(8,128)(2,1)}, u32[]{:S(2)}) copy-start(bf16[2,128,512]{2,1,0:T(8,128)(2,1)} %param.12) | copy-start | bytes 786436
  6.5 119.7 %all-gather.3.cloned.1.call-start = ((), (), s32[]{:S(2)}) async-start(), calls=%async_computation.7 | async-start | bytes 2621440 | tf_op jit(solution)/shard_map/all_gather | solution.py:52
  129.4 12.9 %copy-start.3 = (f32[2,128]{1,0:T(2,128)S(1)}, f32[2,128]{1,0:T(2,128)}, u32[]{:S(2)}) copy-start(f32[2,128]{1,0:T(2,128)} %param.14) | copy-start | bytes 3076
  134.3 38.3 %all-to-all-start.3 = ((bf16[128,2,1024]{2,1,0:T(2,128)(2,1)}), bf16[128,2,1024]{2,1,0:T(2,128)(2,1)S(1)}, u32[]{:S(2)}, u32[]{:S(2)}) async-start(bf16[128,2,1024]{2,1,0:T(2,128)(2,1)} %reshape.206), calls=%async_computation.3 | async-start | bytes 1048576 | tf_op jit(solution)/shard_map/all_to_all | solution.py:63
  142.3 118.1 %all-gather.5.cloned.1.call-start = ((), (), s32[]{:S(2)}) async-start(), calls=%async_computation.8 | async-start | bytes 2621440 | tf_op jit(solution)/shard_map/all_gather | solution.py:59
  173.0 0.8 copy-start.1
  173.2 1.0 copy-start.4
  268.4 45.3 %all-to-all-start.6 = ((bf16[128,2,1024]{2,1,0:T(2,128)(2,1)}), bf16[128,2,1024]{2,1,0:T(2,128)(2,1)S(1)}, u32[]{:S(2)}, u32[]{:S(2)}) async-start(bf16[128,2,1024]{2,1,0:T(2,128)(2,1)} %reshape.208), calls=%async_computation.6 | async-start | bytes 1048576 | tf_op jit(solution)/shard_map/all_to_all | solution.py:63
Sparse Core Ops, SparseCore 0:
  64.0 36.2 all-gather.2
  218.5 36.7 all-gather.4
where the time goes:
time: 326 us; the launch traced here: 324 us
  blocking collectives  191 us (59%)
  waiting for transfers between devices  62.2 us (19%)
  starting transfers between devices  21.1 us (6%)
  other arithmetic  16.2 us (5%)
  between operations  13.8 us (4%)
  local copies, waits for them, and re-layouts  11.4 us (3%)
  matrix products  8.12 us (2%)
    all_to_all x2, blocking collectives, update(): lax.all_to_all(left_op, 'dap', split_axis=0, concat_axis=1, tiled=True)  93.5 us
    all_to_all x2, blocking collectives, update(): lax.all_to_all(right_op, 'dap', split_axis=0, concat_axis=1, tiled=True)  82.7 us
    all_to_all x2, waiting for transfers between devices, update(): lax.all_to_all(triangle.astype(jnp.bfloat16), 'dap', split_axis=1, concat...  62.1 us
    all_to_all x2, starting transfers between devices, update(): lax.all_to_all(triangle.astype(jnp.bfloat16), 'dap', split_axis=1, concat...  21.1 us
    all_to_all x1, blocking collectives, column_rows(): lax.all_to_all(right_chan, 'grp', split_axis=1, concat_axis=2, tiled=True)  14.7 us
    unnamed x3, other arithmetic  11.7 us
  transfers between devices with their start and end apart: 4, of which 2 were waited for; matrix products, arithmetic and copies ran while one was open for 2% of the time, Pallas kernels for 0%

commit v1 on v0

--- a/solution.py
+++ b/solution.py
@@ -1,9 +1,15 @@
+import functools
+
 import jax
 import jax.numpy as jnp
 from jax import lax
+from jax.experimental import pallas as pl
+from jax.experimental.pallas import tpu as pltpu
 from jax.sharding import PartitionSpec as P
 
 epsilon_norm = 1e-05
+MESH = pl.DeviceIdType.MESH
+Z = 16
 
 
 def residue_valid(chain_ids, crop_lengths):
@@ -24,12 +30,72 @@
     return (values - centre) * lax.rsqrt(spread + epsilon_norm) * gain
 
 
+def exchange_kernel(n, x_ref, o_ref, send_sem, recv_sem, own_sem):
+    me = lax.axis_index("dap")
+    planes = n // Z
+    z, plane = me % Z, me // Z
+
+    def partner(step):
+        return ((plane + step // Z) % planes) * Z + (z + step) % Z
+
+    barrier = pltpu.get_barrier_semaphore()
+
+    def greet(step, carry):
+        pl.semaphore_signal(barrier, inc=1, device_id={"dap": partner(step)}, device_id_type=MESH)
+        return carry
+
+    lax.fori_loop(1, n, greet, 0)
+    own = pltpu.make_async_copy(x_ref.at[me], o_ref.at[me], own_sem)
+    own.start()
+    pl.semaphore_wait(barrier, n - 1)
+
+    def send(step, carry):
+        other = partner(step)
+        pltpu.make_async_remote_copy(
+            src_ref=x_ref.at[other],
+            dst_ref=o_ref.at[me],
+            send_sem=send_sem,
+            recv_sem=recv_sem,
+            device_id={"dap": other},
+            device_id_type=MESH,
+        ).start()
+        return carry
+
+    lax.fori_loop(1, n, send, 0)
+    own.wait()
+    everything = pltpu.make_async_remote_copy(
+        src_ref=x_ref.at[pl.ds(0, n - 1)],
+        dst_ref=o_ref.at[pl.ds(0, n - 1)],
+        send_sem=send_sem,
+        recv_sem=recv_sem,
+        device_id={"dap": me},
+        device_id_type=MESH,
+    )
+    everything.wait()
+
+
+def exchange(x, collective_id):
+    n = x.shape[0]
+    return pl.pallas_call(
+        functools.partial(exchange_kernel, n),
+        out_shape=jax.ShapeDtypeStruct(x.shape, x.dtype),
+        in_specs=[pl.BlockSpec(memory_space=pltpu.VMEM)],
+        out_specs=pl.BlockSpec(memory_space=pltpu.VMEM),
+        scratch_shapes=[pltpu.SemaphoreType.DMA, pltpu.SemaphoreType.DMA, pltpu.SemaphoreType.DMA],
+        compiler_params=pltpu.CompilerParams(
+            collective_id=collective_id, has_side_effects=True, vmem_limit_bytes=16 << 20
+        ),
+        name="exchange%d" % collective_id,
+    )(x)
+
+
 def column_rows(right_chan):
-    return lax.all_to_all(right_chan, "grp", split_axis=1, concat_axis=2, tiled=True)
+    return lax.all_to_all(right_chan, "grp", split_axis=0, concat_axis=1, tiled=True)
 
 
 def update(pair_tile, pair_mask, ln_in, w_proj, w_gate, ln_out, w_out, outgoing):
     hidden = w_out.shape[0]
+    rows, columns, _ = pair_tile.shape
     normed = layer_norm(pair_tile.astype(jnp.float32), ln_in, 2).astype(jnp.bfloat16)
     projected = jnp.einsum("rqc,cf->frq", normed, w_proj, preferred_element_type=jnp.float32)
     gate_value = jax.nn.sigmoid(
@@ -41,28 +107,24 @@
     right_op = (
         jax.nn.sigmoid(projected[2 * hidden : 3 * hidden]) * projected[3 * hidden :] * pair_mask
     ).astype(jnp.bfloat16)
-    left_chan, right_chan = (
-        lax.all_to_all(left_op, "dap", split_axis=0, concat_axis=1, tiled=True),
-        lax.all_to_all(right_op, "dap", split_axis=0, concat_axis=1, tiled=True),
+    both = jnp.concatenate(
+        [left_op[:, :, :128], left_op[:, :, 128:], right_op[:, :, :128], right_op[:, :, 128:]], axis=1
     )
+    got = exchange(both, 0)
+    left_chan = jnp.concatenate([got[:, :rows], got[:, rows : 2 * rows]], axis=2).reshape(-1, columns)
+    right_chan = jnp.concatenate(
+        [got[:, 2 * rows : 3 * rows], got[:, 3 * rows :]], axis=2
+    ).reshape(-1, columns)
+    left_all = lax.all_gather(left_chan, "grp", axis=1, tiled=True)
     if outgoing:
-        right_rows = column_rows(right_chan)
         triangle = jnp.einsum(
-            "hik,hjk->hij",
-            lax.all_gather(left_chan, "grp", axis=2, tiled=True),
-            right_rows,
-            preferred_element_type=jnp.float32,
+            "ik,jk->ij", left_all, column_rows(right_chan), preferred_element_type=jnp.float32
         )
     else:
-        triangle = jnp.einsum(
-            "hki,hkj->hij",
-            lax.all_gather(left_chan, "grp", axis=2, tiled=True),
-            right_chan,
-            preferred_element_type=jnp.float32,
-        )
-    returned = lax.all_to_all(
-        triangle.astype(jnp.bfloat16), "dap", split_axis=1, concat_axis=0, tiled=True
-    )
+        triangle = jnp.einsum("ki,kj->ij", left_all, right_chan, preferred_element_type=jnp.float32)
+    triangle = triangle.astype(jnp.bfloat16).reshape(-1, rows, columns)
+    back = exchange(jnp.concatenate([triangle[:, :, :128], triangle[:, :, 128:]], axis=1), 1)
+    returned = jnp.concatenate([back[:, :rows], back[:, rows:]], axis=2)
     normed_product = layer_norm(returned.astype(jnp.float32), ln_out[:, None, None], 0).astype(
         jnp.bfloat16
     )

time: 326 us -> 335 us (1.028)
  Pallas kernels: 0 us -> 212 us
  blocking collectives: 191 us -> 0 us
  starting transfers between devices: 21.1 us -> 6.08 us
  other arithmetic: 16.2 us -> 9.86 us
  local copies, waits for them, and re-layouts: 11.4 us -> 15.9 us
  matrix products: 8.12 us -> 11.9 us
  waiting for transfers between devices: 62.2 us -> 65.7 us
    pallas_call x0 -> x4, Pallas kernels: none -> 212 us  [exchange(): pl.pallas_call(functools.partial(exchange_kernel, n), out_shape=jax.Shape...]
    all_to_all x5 -> x0, blocking collectives: 191 us -> none  [the longest x2 93.5 us: update(): lax.all_to_all(left_op, 'dap', split_axis=0, concat_axis=1, tiled=True)]
    all_gather x2, waiting for transfers between devices: 0.02 us -> 57.7 us  [update(): left_all = lax.all_gather(left_chan, 'grp', axis=1, tiled=True)]
    all_to_all x2 -> x1, waiting for transfers between devices: 62.1 us -> 7.97 us  [column_rows(): lax.all_to_all(right_chan, 'grp', split_axis=0, concat_axis=1, tiled=True)]
    all_to_all x2 -> x1, starting transfers between devices: 21.1 us -> 6.08 us  [column_rows(): lax.all_to_all(right_chan, 'grp', split_axis=0, concat_axis=1, tiled=True)]
    unnamed x3 -> x0, other arithmetic: 11.7 us -> none
    dot_general x0 -> x2, local copies, waits for them, and re-layouts: none -> 10.9 us  [update(): jnp.einsum('rqc,cf->frq', normed, w_proj, preferred_element_type=jnp.floa...]
    convert_element_type x1 -> x2, other arithmetic: 0.58 us -> 5.49 us  [update(): left_op = (jax.nn.sigmoid(projected[:hidden]) * projected[hidden:2 * hidd...]
  transfers between devices with their start and end apart: 4 -> 3, of which waited for: 2 -> 3; matrix products, arithmetic and copies ran while one was open for 2% -> 0% of each run, Pallas kernels for 0% -> 0%
where the time goes in v1:
time: 335 us
  Pallas kernels  212 us (63%)
  waiting for transfers between devices  65.7 us (20%)
  local copies, waits for them, and re-layouts  15.9 us (5%)
  between operations  13.7 us (4%)
  matrix products  11.9 us (4%)
  other arithmetic  9.86 us (3%)
  starting transfers between devices  6.08 us (2%)
    pallas_call x4, Pallas kernels, exchange(): pl.pallas_call(functools.partial(exchange_kernel, n), out_shape=jax.Shape...  212 us
    all_gather x2, waiting for transfers between devices, update(): left_all = lax.all_gather(left_chan, 'grp', axis=1, tiled=True)  57.7 us
    dot_general x2, local copies, waits for them, and re-layouts, update(): jnp.einsum('rqc,cf->frq', normed, w_proj, preferred_element_type=jnp.floa...  10.9 us
    all_to_all x1, waiting for transfers between devices, column_rows(): lax.all_to_all(right_chan, 'grp', split_axis=0, concat_axis=1, tiled=True)  7.97 us
  transfers between devices with their start and end apart: 3, of which 3 were waited for; matrix products, arithmetic and copies ran while one was open for 0% of the time, Pallas kernels for 0%

profile of v1, /device:TPU:25, one launch (start us, length us, event | category | flops | bytes accessed | tf_op | source)
XLA Modules:
  0.0 334.9 jit_solution(17994000751887537433)
XLA Ops:
  6.5 0.0 copy-start
  6.5 0.0 all-gather.3.cloned.1.call-start
  6.5 1.3 copy.38
  7.8 0.8 slice_bitcast_fusion.1
  8.6 0.1 convert_reduce_fusion.1
  8.7 0.2 fusion.23
  8.9 0.0 copy-done
  8.9 2.7 fusion.52
  11.6 0.0 copy-start.2
  11.6 0.0 copy-start.4
  11.6 5.5 %copy.42 = f32[8,256,512]{1,0,2:T(8,128)} copy(f32[8,256,512]{2,1,0:T(8,128)} %fusion.52) | data formatting | bytes 8388608 | tf_op jit(solution)/shard_map/rqc,cf->frq/dot_general | solution.py:100
  17.1 0.0 copy-done.2
  17.1 0.1 convert_reduce_fusion.4
  17.2 0.2 reduce-window.8
  17.4 0.0 copy-done.4
  17.4 0.1 select_reduce_fusion.1
  17.5 0.1 dynamic_slice.7
  17.6 0.1 dynamic_slice.6
  17.7 0.1 broadcast_multiply_fusion
  17.7 2.7 fusion.48
  20.5 0.2 fusion.98
  20.7 0.2 pad_maximum_fusion.x_ref
  20.9 66.8 %exchange0.2 = bf16[128,32,128]{2,1,0:T(8,128)(2,1)S(1)} custom-call(bf16[128,32,128]{2,1,0:T(8,128)(2,1)S(1)} %pad_maximum_fusion.x_ref), custom_call_target="tpu_custom_call" | custom-call | tf_op jit(solution)/shard_map/exchange0/pallas_call | solution.py:79
  87.6 0.2 fusion.91
  87.8 0.9 maximum_bitcast_fusion
  88.7 0.0 all-gather.3.cloned.1.call-update
  88.7 0.1 pad_maximum_fusion.2
  88.8 1.0 copy.43
  89.8 6.1 %all-to-all-start = ((bf16[4,256,256]{1,2,0:T(8,128)(2,1)}), bf16[4,256,256]{1,2,0:T(8,128)(2,1)S(1)}, u32[]{:S(2)}, u32[]{:S(2)}) async-start(bf16[4,256,256]{1,2,0:T(8,128)(2,1)} %copy.43), calls=%async_computation | async-start | bytes 1048576 | tf_op jit(solution)/shard_map/all_to_all | solution.py:93
  95.9 0.0 all-gather.5.cloned.1.call-start
  95.9 0.0 copy-done.3
  95.9 8.0 %all-to-all-done = bf16[4,256,256]{1,2,0:T(8,128)(2,1)S(1)} async-done(((bf16[4,256,256]{1,2,0:T(8,128)(2,1)}), bf16[4,256,256]{1,2,0:T(8,128)(2,1)S(1)}, u32[]{:S(2)}, u32[]{:S(2)}) %all-to-all-start) | async-done | bytes 524320 | tf_op jit(solution)/shard_map/all_to_all | solution.py:93
  103.8 21.9 %all-gather.3.cloned.1.call-done = bf16[1024,1024]{1,0:T(8,128)(2,1)} async-done(((bf16[1024,256]{1,0:T(8,128)(2,1)}), bf16[1024,1024]{1,0:T(8,128)(2,1)}) %all-gather.3.cloned.1.call-update) | async-done | bytes 2097168 | tf_op jit(solution)/shard_map/all_gather | solution.py:118
  125.7 2.3 fusion.18
  128.1 0.1 pad_maximum_fusion.3.x_ref
  128.2 0.0 copy-start.1
  128.2 41.8 %exchange1.2 = bf16[128,16,128]{2,1,0:T(8,128)(2,1)S(1)} custom-call(bf16[128,16,128]{2,1,0:T(8,128)(2,1)S(1)} %pad_maximum_fusion.3.x_ref), custom_call_target="tpu_custom_call" | custom-call | tf_op jit(solution)/shard_map/exchange1/pallas_call | solution.py:79
  170.0 0.0 copy-start.5
  170.1 0.2 convert_reduce_fusion.3
  170.2 0.2 fusion.29
  170.4 0.2 fusion.31
  170.7 0.0 copy-done.1
  170.7 0.3 fusion.62
  171.0 0.0 copy-done.5
  171.0 0.6 convert_reduce_fusion
  171.6 0.2 fusion.20
  171.8 2.7 fusion.55
  174.5 5.4 %copy.49 = f32[8,256,512]{1,0,2:T(8,128)} copy(f32[8,256,512]{2,1,0:T(8,128)} %fusion.55) | data formatting | bytes 8388608 | tf_op jit(solution)/shard_map/rqc,cf->frq/dot_general | solution.py:100
  179.9 2.7 fusion.38
  182.8 0.2 pad_maximum_fusion.1.x_ref
  183.0 61.5 %exchange0.3 = bf16[128,32,128]{2,1,0:T(8,128)(2,1)S(1)} custom-call(bf16[128,32,128]{2,1,0:T(8,128)(2,1)S(1)} %pad_maximum_fusion.1.x_ref), custom_call_target="tpu_custom_call" | custom-call | tf_op jit(solution)/shard_map/exchange0/pallas_call | solution.py:79
  244.4 0.2 fusion.90
  244.6 0.9 maximum_bitcast_fusion.1
  245.5 0.0 all-gather.5.cloned.1.call-update
  245.5 35.8 %all-gather.5.cloned.1.call-done = bf16[1024,1024]{1,0:T(8,128)(2,1)} async-done(((bf16[1024,256]{1,0:T(8,128)(2,1)}), bf16[1024,1024]{1,0:T(8,128)(2,1)}) %all-gather.5.cloned.1.call-update) | async-done | bytes 2097168 | tf_op jit(solution)/shard_map/all_gather | solution.py:118
  281.4 2.3 fusion.19
  283.8 0.1 pad_maximum_fusion.5.x_ref
  283.9 41.7 %exchange1.3 = bf16[128,16,128]{2,1,0:T(8,128)(2,1)S(1)} custom-call(bf16[128,16,128]{2,1,0:T(8,128)(2,1)S(1)} %pad_maximum_fusion.5.x_ref), custom_call_target="tpu_custom_call" | custom-call | tf_op jit(solution)/shard_map/exchange1/pallas_call | solution.py:79
  325.6 0.2 convert_reduce_fusion.2
  325.8 0.2 fusion.26
  326.0 0.2 fusion.28
  326.2 0.3 fusion.60
  326.5 0.6 fusion.9
  327.1 1.0 copy.52
  (18 shorter events, 0.3 us)
Async XLA Ops:
  6.5 2.3 copy-start
  6.5 119.2 %all-gather.3.cloned.1.call-start = ((), (), s32[]{:S(2)}) async-start(), calls=%async_computation.1 | async-start | bytes 2621440 | tf_op jit(solution)/shard_map/all_gather | solution.py:118
  11.6 5.5 %copy-start.2 = (s32[1024]{0:T(1024)S(1)}, s32[1024]{0:T(1024)}, u32[]{:S(2)}) copy-start(s32[1024]{0:T(1024)} %param.9) | copy-start | bytes 12292
  11.6 5.8 %copy-start.4 = (s32[8]{0:T(128)S(1)}, s32[8]{0:T(128)}, u32[]{:S(2)}) copy-start(s32[8]{0:T(128)} %param.10) | copy-start | bytes 100
  88.7 7.2 %copy-start.3 = (f32[2,128]{1,0:T(2,128)S(1)}, f32[2,128]{1,0:T(2,128)}, u32[]{:S(2)}) copy-start(f32[2,128]{1,0:T(2,128)} %param.14) | copy-start | bytes 3076
  89.8 14.1 %all-to-all-start = ((bf16[4,256,256]{1,2,0:T(8,128)(2,1)}), bf16[4,256,256]{1,2,0:T(8,128)(2,1)S(1)}, u32[]{:S(2)}, u32[]{:S(2)}) async-start(bf16[4,256,256]{1,2,0:T(8,128)(2,1)} %copy.43), calls=%async_computation | async-start | bytes 1048576 | tf_op jit(solution)/shard_map/all_to_all | solution.py:93
  95.9 185.5 %all-gather.5.cloned.1.call-start = ((), (), s32[]{:S(2)}) async-start(), calls=%async_computation.2 | async-start | bytes 2621440 | tf_op jit(solution)/shard_map/all_gather | solution.py:118
  128.2 42.5 %copy-start.1 = (bf16[2,128,128]{2,1,0:T(8,128)(2,1)S(1)}, bf16[2,128,128]{2,1,0:T(8,128)(2,1)}, u32[]{:S(2)}) copy-start(bf16[2,128,128]{2,1,0:T(8,128)(2,1)} %param.15) | copy-start | bytes 196612
  170.0 0.9 copy-start.5
Sparse Core Ops, SparseCore 0:
  88.8 36.8 all-gather.2
  245.6 35.6 all-gather.4

commit v2 on v0

v2 whole, which is shorter than its diff:
```python
import functools

import jax
import jax.numpy as jnp
from jax import lax
from jax.experimental import pallas as pl
from jax.experimental.pallas import tpu as pltpu
from jax.sharding import PartitionSpec as P

epsilon_norm = 1e-05
MESH = pl.DeviceIdType.MESH
F32, BF16 = jnp.float32, jnp.bfloat16
Z = 16
PLANES = 8
DAP = Z * PLANES
GRP = 4
GROUPS = 4
SLOTS = DAP // GROUPS
ROWS, COLS, CHAN = 8, 256, 128
BLOCK = SLOTS * ROWS


def residue_valid(chain_ids, crop_lengths):
    count = chain_ids.shape[0]
    chains = jnp.arange(crop_lengths.shape[0], dtype=jnp.int32)
    member = (chain_ids[:, None] == chains[None, :]).astype(jnp.int32)
    counts = jnp.sum(member, axis=0)
    starts = jnp.cumsum(counts) - counts
    first = jnp.sum(member * starts[None, :], axis=1)
    limit = jnp.sum(member * crop_lengths[None, :], axis=1)
    place = jnp.arange(count, dtype=jnp.int32) - first
    return (place < limit).astype(jnp.float32)


def sigmoid(v):
    return 0.5 * jnp.tanh(0.5 * v) + 0.5


def kernel(
    pair_ref, mask_ref, gain_in_ref, w_proj_ref, w_gate_ref, gain_out_ref, w_out_ref,
    out_ref,
    pair_t, normed, gate, staged, right_src, left_src, right_got, left_got,
    right_own, right_mates, left_all, total, tri_src, tri_got, product,
    own_sem, send_sem, right_sem, left_sem, right_mate_sem, left_mate_sem, tri_sem,
):
    me, grp = lax.axis_index("dap"), lax.axis_index("grp")
    z, plane = me % Z, me // Z

    def spot(slot):
        p = slot // PLANES
        half = p // 2
        return 8 + half - (p % 2) * (2 * half + 1), PLANES - 1 - slot % PLANES

    def target(slot):
        along, across = spot(slot)
        return ((plane + across) % PLANES) * Z + (z + along) % Z

    def origin(slot):
        along, across = spot(slot)
        return ((plane + PLANES - across) % PLANES) * Z + (z + Z - along) % Z

    def remote(src, dst, send, recv, dap=None, mate=None):
        device = {"dap": dap} if mate is None else {"grp": mate}
        return pltpu.make_async_remote_copy(
            src_ref=src,
            dst_ref=dst,
            send_sem=send_sem.at[send],
            recv_sem=recv,
            device_id=device,
            device_id_type=MESH,
        )

    def each(lo, hi, body):
        def step(i, carry):
            body(i)
            return carry

        lax.fori_loop(lo, hi, step, 0)

    barrier = pltpu.get_barrier_semaphore()

    def greet(slot):
        pl.semaphore_signal(barrier, inc=1, device_id={"dap": target(slot)}, device_id_type=MESH)

    each(0, DAP - 1, greet)
    for turn in range(1, GRP):
        pl.semaphore_signal(barrier, inc=1, device_id={"grp": (grp + turn) % GRP}, device_id_type=MESH)

    def turn_in(r):
        pair_t[r] = pair_ref[r].astype(F32).T.astype(BF16)

    each(0, ROWS, turn_in)

    def normalise(u):
        def row(r):
            x = pair_t[r].astype(F32)
            centred = x - jnp.mean(x, axis=0, keepdims=True)
            spread = jnp.mean(centred * centred, axis=0, keepdims=True)
            normed[r] = (centred * lax.rsqrt(spread + epsilon_norm) * gain_in_ref[u]).astype(BF16)

        each(0, ROWS, row)

    def operand(u, which, src):
        def row(r):
            both = jnp.dot(w_proj_ref[u, which], normed[r], preferred_element_type=F32)
            value = sigmoid(both[:CHAN]) * both[CHAN:] * mask_ref[pl.ds(r, 1), :]
            staged[pl.ds(r, CHAN, stride=2 * ROWS), :] = value[:, :128]
            staged[pl.ds(ROWS + r, CHAN, stride=2 * ROWS), :] = value[:, 128:]

        each(0, ROWS, row)

        def pack(i):
            rows = staged[pl.ds(pl.multiple_of(i * 256, 256), 256), :]
            src[pl.ds(i * 16, 16)] = rows.reshape(16, 16, 128).astype(BF16)

        each(0, 8, pack)

    def gates(u):
        def row(r):
            gate[r] = sigmoid(jnp.dot(w_gate_ref[u], normed[r], preferred_element_type=F32))

        each(0, ROWS, row)

    def unpack(got, first, dst, row0):
        def some(i):
            tiles = got[pl.ds(first + i * 8, 8)].astype(F32)
            at = pl.ds(pl.multiple_of(row0 + i * 64, 64), 64)
            dst[at, 0:128] = tiles[:, :ROWS].reshape(64, 128).astype(BF16)
            dst[at, 128:256] = tiles[:, ROWS:].reshape(64, 128).astype(BF16)

        each(0, SLOTS // 8, some)

    def send_relative(src, got, send, sems, own):
        for k in range(GROUPS):
            def one(slot):
                other = target(slot)
                remote(src.at[other], got.at[slot], send, sems.at[k], dap=other).start()

            each(k * SLOTS, min((k + 1) * SLOTS, DAP - 1), one)
        pltpu.make_async_copy(src.at[me], got.at[DAP - 1], own).start()

    def wait_group(src, got, sems, own, k):
        count = SLOTS - (k == GROUPS - 1)
        remote(src.at[pl.ds(0, count)], got.at[pl.ds(0, count)], 0, sems.at[k], dap=me).wait_recv()
        if k == GROUPS - 1:
            pltpu.make_async_copy(src.at[me], got.at[DAP - 1], own).wait()

    def sent(src, send):
        everything = src.at[pl.ds(0, DAP - 1)]
        remote(everything, everything, send, tri_sem.at[0], dap=me).wait_send()

    def all_sent(u):
        sent(right_src, 0)
        sent(left_src, 1)
        sent(tri_src, 2)
        shared = left_all.at[u, :, pl.ds(0, GRP - 1)]
        remote(shared, shared, 4, tri_sem.at[0], mate=grp).wait_send()

    def pack_triangle(values, first):
        halves = [values[:, :128].reshape(SLOTS, ROWS, 128), values[:, 128:].reshape(SLOTS, ROWS, 128)]
        tri_src[pl.ds(first, SLOTS)] = jnp.concatenate(halves, axis=1).astype(BF16)

    def finish(u, last):
        remote(
            tri_src.at[pl.ds(0, DAP - 1)], tri_got.at[u, pl.ds(0, DAP - 1)], 2, tri_sem.at[u], dap=me
        ).wait_recv()
        for s in range(2):
            x = tri_got[u, :, s * ROWS : (s + 1) * ROWS].astype(F32)
            centred = x - jnp.mean(x, axis=0, keepdims=True)
            spread = jnp.mean(centred * centred, axis=0, keepdims=True)
            product[s] = (centred * lax.rsqrt(spread + epsilon_norm)).reshape(CHAN * ROWS, 128)

        def row(r):
            across = [product[s, pl.ds(r, CHAN, stride=ROWS), :] for s in range(2)]
            scaled = (jnp.concatenate(across, axis=1) * gain_out_ref[u]).astype(BF16)
            term = jnp.dot(w_out_ref[u], scaled, preferred_element_type=F32)
            result = pair_t[r].astype(F32) + gate[r] * term
            if last:
                out_ref[r] = result.T.astype(BF16)
            else:
                pair_t[r] = result.astype(BF16)

        each(0, ROWS, row)

    normalise(0)
    operand(0, 1, right_src)
    pl.semaphore_wait(barrier, DAP - 1 + GRP - 1)

    def send_right(slot):
        other = target(slot)
        remote(right_src.at[other], right_got.at[0, me], 0, right_sem.at[GROUPS], dap=other).start()

    each(0, DAP - 1, send_right)
    pltpu.make_async_copy(right_src.at[me], right_got.at[0, me], own_sem.at[0]).start()
    operand(0, 0, left_src)
    send_relative(left_src, left_got.at[0], 1, left_sem.at[0], own_sem.at[1])
    gates(0)
    pltpu.make_async_copy(right_src.at[me], right_got.at[0, me], own_sem.at[0]).wait()
    remote(
        right_src.at[pl.ds(0, DAP - 1)], right_got.at[0, pl.ds(0, DAP - 1)], 0, right_sem.at[GROUPS], dap=me
    ).wait_recv()
    for k in range(GRP):
        unpack(right_got.at[0], k * SLOTS, right_own.at[k], 0)
    for turn in range(1, GRP):
        mate = (grp + turn) % GRP
        remote(right_own.at[mate], right_mates.at[grp], 3, right_mate_sem, mate=mate).start()
    right_mates[grp] = right_own[grp]

    def share_left(u, k):
        for turn in range(1, GRP):
            mate = (grp + turn) % GRP
            remote(left_all.at[u, k, grp], left_all.at[u, k, grp], 4, left_mate_sem.at[u, k], mate=mate).start()

    def wait_mates(u, k):
        three = left_all.at[u, k, pl.ds(0, GRP - 1)]
        remote(three, three, 4, left_mate_sem.at[u, k], mate=grp).wait_recv()

    def take_left(k):
        wait_group(left_src, left_got.at[0], left_sem.at[0], own_sem.at[1], k)
        unpack(left_got.at[0], k * SLOTS, left_all.at[0, k, grp], 0)
        share_left(0, k)

    def return_rows(k):
        wait_mates(0, k)
        value = jnp.zeros((BLOCK, COLS), F32)
        for q in range(GRP):
            value += lax.dot_general(
                left_all[0, k, q], right_mates[q], (((1,), (1,)), ((), ())), preferred_element_type=F32
            )
        pack_triangle(value, k * SLOTS)

        def one(slot):
            remote(tri_src.at[slot], tri_got.at[0, me], 2, tri_sem.at[0], dap=origin(slot)).start()

        each(k * SLOTS, min((k + 1) * SLOTS, DAP - 1), one)

    take_left(0)
    three = right_mates.at[pl.ds(0, GRP - 1)]
    remote(three, three, 3, right_mate_sem, mate=grp).wait_recv()
    for k in range(1, GROUPS):
        take_left(k)
        return_rows(k - 1)
    return_rows(GROUPS - 1)
    own_triangle = pltpu.make_async_copy(tri_src.at[DAP - 1], tri_got.at[0, me], own_sem.at[2])
    own_triangle.start()
    own_triangle.wait()
    finish(0, False)
    all_sent(0)
    remote(three, three, 3, right_mate_sem, mate=grp).wait_send()

    normalise(1)
    operand(1, 0, left_src)
    send_relative(left_src, left_got.at[1], 1, left_sem.at[1], own_sem.at[3])
    operand(1, 1, right_src)
    send_relative(right_src, right_got.at[1], 0, right_sem, own_sem.at[4])
    gates(1)
    for k in range(GROUPS):
        wait_group(left_src, left_got.at[1], left_sem.at[1], own_sem.at[3], k)
        unpack(left_got.at[1], k * SLOTS, right_own.at[0], 0)
        left_all[1, k, grp] = right_own[0].astype(F32).T.astype(BF16)
        share_left(1, k)
    for k in range(GROUPS):
        wait_group(right_src, right_got.at[1], right_sem, own_sem.at[4], k)
        unpack(right_got.at[1], k * SLOTS, right_own.at[1], 0)
        wait_mates(1, k)
        for q in range(GRP):
            part = jnp.dot(left_all[1, k, q], right_own[1], preferred_element_type=F32)
            if k == 0:
                total[q] = part
            elif k < GROUPS - 1:
                total[q] += part
            else:
                pack_triangle(total[q] + part, q * SLOTS)

    def send_back(slot):
        other = target(slot)
        remote(tri_src.at[other], tri_got.at[1, me], 2, tri_sem.at[1], dap=other).start()

    each(0, DAP - 1, send_back)
    own_triangle = pltpu.make_async_copy(tri_src.at[me], tri_got.at[1, me], own_sem.at[5])
    own_triangle.start()
    own_triangle.wait()
    finish(1, True)
    all_sent(1)


def shards(pair_rep, chain_ids, crop_lengths, ln_in_gain, w_proj, w_gate, ln_out_gain, w_out):
    kept = residue_valid(chain_ids, crop_lengths)
    kept_rows = lax.dynamic_slice_in_dim(kept, lax.axis_index("dap") * ROWS, ROWS, 0)
    kept_columns = lax.dynamic_slice_in_dim(kept, lax.axis_index("grp") * COLS, COLS, 0)
    pair_mask = kept_rows[:, None] * kept_columns[None, :]
    w_proj_t = w_proj.transpose(0, 2, 1).reshape(2, 2, 2 * CHAN, CHAN)
    vmem = pl.BlockSpec(memory_space=pltpu.VMEM)
    tiles = (DAP, 2 * ROWS, 128)
    return pl.pallas_call(
        kernel,
        out_shape=jax.ShapeDtypeStruct(pair_rep.shape, BF16),
        in_specs=[vmem] * 7,
        out_specs=vmem,
        scratch_shapes=[
            pltpu.VMEM((ROWS, CHAN, COLS), BF16),
            pltpu.VMEM((ROWS, CHAN, COLS), BF16),
            pltpu.VMEM((ROWS, CHAN, COLS), F32),
            pltpu.VMEM((CHAN * 2 * ROWS, 128), F32),
            pltpu.VMEM(tiles, BF16),
            pltpu.VMEM(tiles, BF16),
            pltpu.VMEM((2,) + tiles, BF16),
            pltpu.VMEM((2,) + tiles, BF16),
            pltpu.VMEM((GRP, BLOCK, COLS), BF16),
            pltpu.VMEM((GRP, BLOCK, COLS), BF16),
            pltpu.VMEM((2, GROUPS, GRP, BLOCK, COLS), BF16),
            pltpu.VMEM((GRP, BLOCK, COLS), F32),
            pltpu.VMEM(tiles, BF16),
            pltpu.VMEM((2,) + tiles, BF16),
            pltpu.VMEM((2, CHAN * ROWS, 128), F32),
            pltpu.SemaphoreType.DMA((6,)),
            pltpu.SemaphoreType.DMA((5,)),
            pltpu.SemaphoreType.DMA((GROUPS + 1,)),
            pltpu.SemaphoreType.DMA((2, GROUPS)),
            pltpu.SemaphoreType.DMA,
            pltpu.SemaphoreType.DMA((2, GROUPS)),
            pltpu.SemaphoreType.DMA((2,)),
        ],
        compiler_params=pltpu.CompilerParams(
            collective_id=0, has_side_effects=True, vmem_limit_bytes=40 << 20
        ),
        name="triangles",
    )(
        pair_rep,
        pair_mask,
        ln_in_gain[:, :, None],
        w_proj_t,
        w_gate.transpose(0, 2, 1),
        ln_out_gain[:, :, None],
        w_out.transpose(0, 2, 1),
    )


def solution(mesh):
    placed = (P("dap", "grp", None), P(), P(), P(), P(), P(), P(), P())
    return jax.shard_map(
        shards, mesh=mesh, in_specs=placed, out_specs=P("dap", "grp", None), check_vma=False
    )
```

time: 326 us -> 187 us (0.57)
  blocking collectives: 191 us -> 0 us
  Pallas kernels: 0 us -> 179 us
  waiting for transfers between devices: 62.2 us -> 0 us
  starting transfers between devices: 21.1 us -> 0 us
  other arithmetic: 16.2 us -> 1.89 us
  between operations: 13.8 us -> 0.1 us
  local copies, waits for them, and re-layouts: 11.4 us -> 2.2 us
  matrix products: 8.12 us -> 0 us
    all_to_all x5 -> x0, blocking collectives: 191 us -> none  [the longest x2 93.5 us: update(): lax.all_to_all(left_op, 'dap', split_axis=0, concat_axis=1, tiled=True)]
    pallas_call x0 -> x1, Pallas kernels: none -> 179 us  [shards(): pl.pallas_call(kernel, out_shape=jax.ShapeDtypeStruct(pair_rep.shape, BF1...]
    all_to_all x2 -> x0, waiting for transfers between devices: 62.1 us -> none  [update(): lax.all_to_all(triangle.astype(jnp.bfloat16), 'dap', split_axis=1, concat...]
    all_to_all x2 -> x0, starting transfers between devices: 21.1 us -> none  [update(): lax.all_to_all(triangle.astype(jnp.bfloat16), 'dap', split_axis=1, concat...]
    unnamed x3 -> x0, other arithmetic: 11.7 us -> none
    dot_general x8 -> x0, matrix products: 8.12 us -> none  [the longest x1 2.35 us: update(): jnp.einsum('hki,hkj->hij', lax.all_gather(left_chan, 'grp', axis=2, tiled...]
    convert_element_type x7 -> x0, local copies, waits for them, and re-layouts: 4.23 us -> none  [the longest x2 1.62 us: update(): triangle.astype(jnp.bfloat16)]
    unnamed x19 -> x15, local copies, waits for them, and re-layouts: 5.63 us -> 1.61 us
  transfers between devices with their start and end apart: 4 -> 0, of which waited for: 2 -> 0; matrix products, arithmetic and copies ran while one was open for 2% -> 0% of each run, Pallas kernels for 0% -> 0%
where the time goes in v2:
time: 187 us; the launch traced here: 184 us
  Pallas kernels  179 us (96%)
  local copies, waits for them, and re-layouts  2.2 us (1%)
  other arithmetic  1.89 us (1%)
    pallas_call x1, Pallas kernels, shards(): pl.pallas_call(kernel, out_shape=jax.ShapeDtypeStruct(pair_rep.shape, BF1...  179 us

profile of v2, /device:TPU:25, one launch (start us, length us, event | category | flops | bytes accessed | tf_op | source)
XLA Modules:
  0.0 183.7 jit_solution(6827413708533234937)
XLA Ops:
  0.0 0.0 copy-start.2
  0.0 0.8 convert_reduce_fusion
  0.8 0.2 reduce-window.8
  1.0 0.8 select_reduce_fusion.1
  1.8 0.0 copy-start.4
  1.8 0.1 dynamic_slice.6
  1.9 0.0 copy-start.3
  1.9 0.1 dynamic_slice.7
  2.0 0.0 copy-start.5
  2.0 0.0 copy-start.1
  2.0 0.1 broadcast_multiply_fusion.mask_ref
  2.1 0.0 copy-done.2
  2.1 0.0 copy-start
  2.1 0.1 copy.18
  2.2 0.6 copy-done.3
  2.8 0.1 copy.19
  2.9 0.0 copy-done.4
  2.9 0.1 copy.20.gain_in_ref
  3.0 0.0 copy-done.5
  3.0 0.1 copy.21.gain_out_ref
  3.2 0.0 copy-done.1
  3.2 0.2 copy.17
  3.4 0.0 copy-done
  3.4 179.5 %triangles.1 = bf16[8,256,128]{2,1,0:T(8,128)(2,1)S(1)} custom-call(bf16[8,256,128]{2,1,0:T(8,128)(2,1)S(1)} %copy-done, f32[8,256]{1,0:T(8,128)S(1)} %broadcast_multiply_fusion.mask_ref, f32[2,128,1]{2,1,0:T(8,128)S(1)} %copy.20.gain_in_ref, bf16[2,2,256,128]{3,2,1,0:T(8,128)(2,1)S(1)} %bitcast.9, bf16[2,128,128]{2,1,0:T(8,128)(2,1)S(1)} %bitcast.10, ...), custom_call_target="tpu_custom_call" | custom-call | tf_op jit(solution)/shard_map/triangles/pallas_call | solution.py:295
  182.9 0.8 copy.23
  (2 shorter events, 0.0 us)
Async XLA Ops:
  0.0 2.1 %copy-start.2 = (bf16[2,128,128]{2,1,0:T(8,128)(2,1)S(1)}, bf16[2,128,128]{2,1,0:T(8,128)(2,1)}, u32[]{:S(2)}) copy-start(bf16[2,128,128]{2,1,0:T(8,128)(2,1)} %param.13) | copy-start | bytes 196612
  1.8 1.1 copy-start.4
  1.9 0.8 copy-start.3
  2.0 1.0 copy-start.5
  2.0 1.2 copy-start.1
  2.1 1.3 copy-start

commit v3 on v2

v3 whole, which is shorter than its diff:
```python
import functools

import jax
import jax.numpy as jnp
from jax import lax
from jax.experimental import pallas as pl
from jax.experimental.pallas import tpu as pltpu
from jax.sharding import PartitionSpec as P

epsilon_norm = 1e-05
MESH = pl.DeviceIdType.MESH
F32, BF16 = jnp.float32, jnp.bfloat16
Z = 16
PLANES = 8
DAP = Z * PLANES
GRP = 4
GROUPS = 4
SLOTS = DAP // GROUPS
ROWS, COLS, CHAN = 8, 256, 128
BLOCK = SLOTS * ROWS
HALF = COLS // 2


def residue_valid(chain_ids, crop_lengths):
    count = chain_ids.shape[0]
    chains = jnp.arange(crop_lengths.shape[0], dtype=jnp.int32)
    member = (chain_ids[:, None] == chains[None, :]).astype(jnp.int32)
    counts = jnp.sum(member, axis=0)
    starts = jnp.cumsum(counts) - counts
    first = jnp.sum(member * starts[None, :], axis=1)
    limit = jnp.sum(member * crop_lengths[None, :], axis=1)
    place = jnp.arange(count, dtype=jnp.int32) - first
    return (place < limit).astype(jnp.float32)


def sigmoid(v):
    return 0.5 * jnp.tanh(0.5 * v) + 0.5


def kernel(
    pair_ref, mask_ref, gain_in_ref, w_proj_ref, w_gate_ref, gain_out_ref, w_out_ref,
    out_ref,
    pair_t, normed, gate, staged, product,
    right_src, left_src, right_got, left_got, right_own, right_mates, left_all, tri_src, tri_got,
    both_src, both_got, late_src, late_got, unpacked, left_t, right_m,
    own_sem, send_sem, right_sem, left_sem, right_mate_sem, left_mate_sem, tri_sem,
    both_sem, late_left_sem, late_right_sem, turned_sem,
):
    me, grp = lax.axis_index("dap"), lax.axis_index("grp")
    z, plane = me % Z, me // Z

    def spot(slot):
        p = slot // PLANES
        half = p // 2
        return 8 + half - (p % 2) * (2 * half + 1), PLANES - 1 - slot % PLANES

    def target(slot):
        along, across = spot(slot)
        return ((plane + across) % PLANES) * Z + (z + along) % Z

    def origin(slot):
        along, across = spot(slot)
        return ((plane + PLANES - across) % PLANES) * Z + (z + Z - along) % Z

    def remote(src, dst, send, recv, dap=None, mate=None):
        device = {"dap": dap} if mate is None else {"grp": mate}
        return pltpu.make_async_remote_copy(
            src_ref=src,
            dst_ref=dst,
            send_sem=send_sem.at[send],
            recv_sem=recv,
            device_id=device,
            device_id_type=MESH,
        )

    def each(lo, hi, body):
        def step(i, carry):
            body(i)
            return carry

        lax.fori_loop(lo, hi, step, 0)

    def received(ref, sem):
        remote(ref, ref, 0, sem, dap=me).wait_recv()

    def sent(ref, send):
        remote(ref, ref, send, right_sem, dap=me).wait_send()

    def own_copy(src, dst, sem):
        return pltpu.make_async_copy(src, dst, own_sem.at[sem])

    barrier = pltpu.get_barrier_semaphore()

    def greet(slot):
        pl.semaphore_signal(barrier, inc=1, device_id={"dap": target(slot)}, device_id_type=MESH)

    each(0, DAP - 1, greet)
    for turn in range(1, GRP):
        pl.semaphore_signal(barrier, inc=1, device_id={"grp": (grp + turn) % GRP}, device_id_type=MESH)

    def turn_in(r):
        for s in range(2):
            pair_t[s, r] = pair_ref[r, s * HALF : (s + 1) * HALF].astype(F32).T.astype(BF16)

    each(0, ROWS, turn_in)

    def normalise(u, s):
        def row(r):
            x = pair_t[s, r].astype(F32)
            centred = x - jnp.mean(x, axis=0, keepdims=True)
            spread = jnp.mean(centred * centred, axis=0, keepdims=True)
            normed[s, r] = (centred * lax.rsqrt(spread + epsilon_norm) * gain_in_ref[u]).astype(BF16)

        each(0, ROWS, row)

    def operand(u, which, s, first, stride):
        def row(r):
            both = jnp.dot(w_proj_ref[u, which], normed[s, r], preferred_element_type=F32)
            value = sigmoid(both[:CHAN]) * both[CHAN:] * mask_ref[s, r]
            staged[pl.ds(first + r, CHAN, stride=stride), :] = value

        each(0, ROWS, row)

    def pack(src, stride):
        def some(i):
            rows = staged[pl.ds(pl.multiple_of(i * 16 * stride, 128), 16 * stride), :]
            src[pl.ds(i * 16, 16)] = rows.reshape(16, stride, 128).astype(BF16)

        each(0, CHAN // 16, some)

    def gates(u, s):
        def row(r):
            gate[s, r] = sigmoid(jnp.dot(w_gate_ref[u], normed[s, r], preferred_element_type=F32))

        each(0, ROWS, row)

    def send_slots(src, got, send, sem_of, lo, hi):
        def one(slot):
            other = target(slot)
            remote(src.at[other], got.at[slot], send, sem_of, dap=other).start()

        each(lo, hi, one)

    def send_groups(src, got, send, sems, own):
        for k in range(GROUPS):
            send_slots(src, got, send, sems.at[k], k * SLOTS, min((k + 1) * SLOTS, DAP - 1))
        own_copy(src.at[me], got.at[DAP - 1], own).start()

    def wait_group(src, got, sems, own, k):
        received(got.at[pl.ds(0, SLOTS - (k == GROUPS - 1))], sems.at[k])
        if k == GROUPS - 1:
            own_copy(src.at[me], got.at[DAP - 1], own).wait()

    def finish(u, s, last):
        received(tri_got.at[u, s, pl.ds(0, DAP - 1)], tri_sem.at[u, s])
        x = tri_got[u, s].astype(F32)
        centred = x - jnp.mean(x, axis=0, keepdims=True)
        spread = jnp.mean(centred * centred, axis=0, keepdims=True)
        product[...] = (centred * lax.rsqrt(spread + epsilon_norm)).reshape(CHAN * ROWS, 128)

        def row(r):
            scaled = (product[pl.ds(r, CHAN, stride=ROWS), :] * gain_out_ref[u]).astype(BF16)
            term = jnp.dot(w_out_ref[u], scaled, preferred_element_type=F32)
            result = pair_t[s, r].astype(F32) + gate[s, r] * term
            if last:
                out_ref[r, s * HALF : (s + 1) * HALF] = result.T.astype(BF16)
            else:
                pair_t[s, r] = result.astype(BF16)

        each(0, ROWS, row)

    for s in range(2):
        normalise(0, s)
        operand(0, 1, s, s * ROWS, 2 * ROWS)
    pack(right_src, 2 * ROWS)
    pl.semaphore_wait(barrier, DAP - 1 + GRP - 1)

    def send_right(slot):
        other = target(slot)
        remote(right_src.at[other], right_got.at[me], 0, right_sem, dap=other).start()

    each(0, DAP - 1, send_right)
    own_copy(right_src.at[me], right_got.at[me], 0).start()
    for s in range(2):
        operand(0, 0, s, s * ROWS, 2 * ROWS)
    pack(left_src, 2 * ROWS)
    send_groups(left_src, left_got, 1, left_sem, 1)
    for s in range(2):
        gates(0, s)

    def unpack_wide(got, first, dst):
        def some(i):
            tiles = got[pl.ds(first + i * 8, 8)].astype(F32)
            at = pl.ds(pl.multiple_of(i * 64, 64), 64)
            dst[at, 0:HALF] = tiles[:, :ROWS].reshape(64, HALF).astype(BF16)
            dst[at, HALF:COLS] = tiles[:, ROWS:].reshape(64, HALF).astype(BF16)

        each(0, SLOTS // 8, some)

    own_copy(right_src.at[me], right_got.at[me], 0).wait()
    received(right_got.at[pl.ds(0, DAP - 1)], right_sem)
    for q in range(GRP):
        unpack_wide(right_got, q * SLOTS, right_own.at[q])
    for turn in range(1, GRP):
        mate = (grp + turn) % GRP
        remote(right_own.at[mate], right_mates.at[grp], 3, right_mate_sem, mate=mate).start()
    right_mates[grp] = right_own[grp]

    def take_left(k):
        wait_group(left_src, left_got, left_sem, 1, k)
        unpack_wide(left_got, k * SLOTS, left_all.at[k, grp])
        for turn in range(1, GRP):
            mate = (grp + turn) % GRP
            remote(left_all.at[k, grp], left_all.at[k, grp], 4, left_mate_sem.at[k], mate=mate).start()

    def rows_of(k):
        received(left_all.at[k, pl.ds(0, GRP - 1)], left_mate_sem.at[k])
        value = jnp.zeros((BLOCK, COLS), F32)
        for q in range(GRP):
            value += lax.dot_general(
                left_all[k, q], right_mates[q], (((1,), (1,)), ((), ())), preferred_element_type=F32
            )
        for s in range(2):
            part = value[:, s * HALF : (s + 1) * HALF].reshape(SLOTS, ROWS, HALF)
            tri_src[0, s, pl.ds(k * SLOTS, SLOTS)] = part.astype(BF16)

    def return_rows(k, s):
        def one(slot):
            remote(tri_src.at[0, s, slot], tri_got.at[0, s, me], 2, tri_sem.at[0, s], dap=origin(slot)).start()

        each(k * SLOTS, min((k + 1) * SLOTS, DAP - 1), one)

    take_left(0)
    received(right_mates.at[pl.ds(0, GRP - 1)], right_mate_sem)
    for k in range(1, GROUPS):
        take_left(k)
        rows_of(k - 1)
        return_rows(k - 1, 0)
    return_rows(0, 1)
    rows_of(GROUPS - 1)
    return_rows(GROUPS - 1, 0)
    for k in range(1, GROUPS):
        return_rows(k, 1)
    for s in range(2):
        own_triangle = own_copy(tri_src.at[0, s, DAP - 1], tri_got.at[0, s, me], 2)
        own_triangle.start()
        own_triangle.wait()

    finish(0, 0, False)
    normalise(1, 0)
    for which in range(2):
        operand(1, which, 0, which * ROWS, 2 * ROWS)
    pack(both_src, 2 * ROWS)
    send_groups(both_src, both_got, 5, both_sem, 3)
    finish(0, 1, False)
    normalise(1, 1)
    operand(1, 0, 1, 0, ROWS)
    pack(late_src.at[0], ROWS)
    send_groups(late_src.at[0], late_got.at[0], 6, late_left_sem, 4)
    operand(1, 1, 1, 0, ROWS)
    pack(late_src.at[1], ROWS)
    send_slots(late_src.at[1], late_got.at[1], 7, late_right_sem, 0, DAP - 1)
    own_copy(late_src.at[1, me], late_got.at[1, DAP - 1], 5).start()
    for s in range(2):
        gates(1, s)

    def unpack(got, first, count, top, dst, row0):
        def some(i):
            tiles = got[pl.ds(first + i * 8, 8)].astype(F32)[:, top : top + ROWS]
            dst[pl.ds(pl.multiple_of(row0 + i * 64, 64), 64), :] = tiles.reshape(64, HALF).astype(BF16)

        each(0, count // 8, some)

    def share_turned(s, k):
        at = pl.ds(k * BLOCK, BLOCK)
        left_t[s, grp, :, at] = unpacked[...].astype(F32).T.astype(BF16)
        for turn in range(1, GRP):
            mate = (grp + turn) % GRP
            part = left_t.at[s, grp, :, at]
            remote(part, part, 8, turned_sem.at[s], mate=mate).start()

    def quadrant(rows_half, s):
        for q in range(GRP):
            value = jnp.dot(left_t[rows_half, q], right_m[s], preferred_element_type=F32)
            first = (2 * q + rows_half) * Z
            tri_src[1, s, pl.ds(first, Z)] = value.reshape(Z, ROWS, HALF).astype(BF16)

    def return_quadrant(rows_half, s):
        odd = (plane + rows_half) % 2

        def one(i):
            along, _ = spot((i // 4) * PLANES)
            across = 2 * (3 - i % 4) + odd
            other = ((plane + across) % PLANES) * Z + (z + along) % Z
            remote(tri_src.at[1, s, other], tri_got.at[1, s, me], 9, tri_sem.at[1, s], dap=other).start()

        each(0, 4 * Z - 1, one)

        @pl.when(odd == 1)
        def _():
            one(4 * Z - 1)

    def keep_own(s):
        own_triangle = own_copy(tri_src.at[1, s, me], tri_got.at[1, s, me], 6)
        own_triangle.start()
        own_triangle.wait()

    for k in range(GROUPS):
        wait_group(both_src, both_got, both_sem, 3, k)
        unpack(both_got, k * SLOTS, SLOTS, 0, unpacked, 0)
        share_turned(0, k)
        unpack(both_got, k * SLOTS, SLOTS, ROWS, right_m.at[0], k * BLOCK)
    received(left_t.at[0, pl.ds(0, GRP - 1)], turned_sem.at[0])
    quadrant(0, 0)
    return_quadrant(0, 0)
    for k in range(GROUPS):
        wait_group(late_src.at[0], late_got.at[0], late_left_sem, 4, k)
        unpack(late_got.at[0], k * SLOTS, SLOTS, 0, unpacked, 0)
        share_turned(1, k)
    received(left_t.at[1, pl.ds(0, GRP - 1)], turned_sem.at[1])
    quadrant(1, 0)
    return_quadrant(1, 0)
    keep_own(0)
    own_copy(late_src.at[1, me], late_got.at[1, DAP - 1], 5).wait()
    received(late_got.at[1, pl.ds(0, DAP - 1)], late_right_sem)
    unpack(late_got.at[1], 0, DAP, 0, right_m.at[1], 0)
    for rows_half in range(2):
        quadrant(rows_half, 1)
        return_quadrant(rows_half, 1)
    keep_own(1)
    finish(1, 0, True)
    finish(1, 1, True)

    most = pl.ds(0, DAP - 1)
    sent(right_src.at[most], 0)
    sent(left_src.at[most], 1)
    sent(right_mates.at[pl.ds(0, GRP - 1)], 3)
    sent(left_all.at[:, pl.ds(0, GRP - 1)], 4)
    sent(both_src.at[most], 5)
    sent(late_src.at[0, most], 6)
    sent(late_src.at[1, most], 7)
    sent(left_t.at[:, pl.ds(0, GRP - 1)], 8)
    sent(tri_src.at[0, :, most], 2)
    sent(tri_src.at[1, :, most], 9)


def shards(pair_rep, chain_ids, crop_lengths, ln_in_gain, w_proj, w_gate, ln_out_gain, w_out):
    kept = residue_valid(chain_ids, crop_lengths)
    kept_rows = lax.dynamic_slice_in_dim(kept, lax.axis_index("dap") * ROWS, ROWS, 0)
    kept_columns = lax.dynamic_slice_in_dim(kept, lax.axis_index("grp") * COLS, COLS, 0)
    pair_mask = kept_rows[None, :, None, None] * kept_columns.reshape(2, 1, 1, HALF)
    w_proj_t = w_proj.transpose(0, 2, 1).reshape(2, 2, 2 * CHAN, CHAN)
    vmem = pl.BlockSpec(memory_space=pltpu.VMEM)
    wide, narrow = (DAP, 2 * ROWS, 128), (DAP, ROWS, 128)
    turned = (2, ROWS, CHAN, HALF)
    square = (BLOCK, COLS)
    dma = pltpu.SemaphoreType.DMA
    return pl.pallas_call(
        kernel,
        out_shape=jax.ShapeDtypeStruct(pair_rep.shape, BF16),
        in_specs=[vmem] * 7,
        out_specs=vmem,
        scratch_shapes=[
            pltpu.VMEM(turned, BF16),
            pltpu.VMEM(turned, BF16),
            pltpu.VMEM(turned, F32),
            pltpu.VMEM((CHAN * 2 * ROWS, 128), F32),
            pltpu.VMEM((CHAN * ROWS, 128), F32),
            pltpu.VMEM(wide, BF16),
            pltpu.VMEM(wide, BF16),
            pltpu.VMEM(wide, BF16),
            pltpu.VMEM(wide, BF16),
            pltpu.VMEM((GRP,) + square, BF16),
            pltpu.VMEM((GRP,) + square, BF16),
            pltpu.VMEM((GROUPS, GRP) + square, BF16),
            pltpu.VMEM((2, 2) + narrow, BF16),
            pltpu.VMEM((2, 2) + narrow, BF16),
            pltpu.VMEM(wide, BF16),
            pltpu.VMEM(wide, BF16),
            pltpu.VMEM((2,) + narrow, BF16),
            pltpu.VMEM((2,) + narrow, BF16),
            pltpu.VMEM((BLOCK, HALF), BF16),
            pltpu.VMEM((2, GRP, HALF, DAP * ROWS), BF16),
            pltpu.VMEM((2, DAP * ROWS, HALF), BF16),
            dma((7,)),
            dma((10,)),
            dma,
            dma((GROUPS,)),
            dma,
            dma((GROUPS,)),
            dma((2, 2)),
            dma((GROUPS,)),
            dma((GROUPS,)),
            dma,
            dma((2,)),
        ],
        compiler_params=pltpu.CompilerParams(
            collective_id=0, has_side_effects=True, vmem_limit_bytes=40 << 20
        ),
        name="triangles",
    )(
        pair_rep,
        pair_mask,
        ln_in_gain[:, :, None],
        w_proj_t,
        w_gate.transpose(0, 2, 1),
        ln_out_gain[:, :, None],
        w_out.transpose(0, 2, 1),
    )


def solution(mesh):
    placed = (P("dap", "grp", None), P(), P(), P(), P(), P(), P(), P())
    return jax.shard_map(
        shards, mesh=mesh, in_specs=placed, out_specs=P("dap", "grp", None), check_vma=False
    )
```

time: 187 us -> 186 us (level); the launches traced: 184 us -> 185 us
  Pallas kernels: 179 us -> 181 us
where the time goes in v3:
time: 186 us; the launch traced here: 185 us
  Pallas kernels  181 us (97%)
  local copies, waits for them, and re-layouts  2.19 us (1%)
  other arithmetic  1.89 us (1%)
    pallas_call x1, Pallas kernels, shards(): pl.pallas_call(kernel, out_shape=jax.ShapeDtypeStruct(pair_rep.shape, BF1...  181 us

profile of v3, /device:TPU:25, one launch (start us, length us, event | category | flops | bytes accessed | tf_op | source)
XLA Modules:
  0.0 185.1 jit_solution(1944707614594454920)
XLA Ops:
  0.0 0.0 copy-start.2
  0.0 0.8 convert_reduce_fusion
  0.8 0.2 reduce-window.8
  1.0 0.8 select_reduce_fusion.1
  1.8 0.0 copy-start.4
  1.8 0.1 dynamic_slice.6
  1.9 0.0 copy-start.3
  1.9 0.1 dynamic-slice_bitcast_fusion
  2.0 0.0 copy-start.5
  2.0 0.0 copy-start.1
  2.0 0.1 broadcast_multiply_fusion.mask_ref
  2.1 0.0 copy-done.2
  2.1 0.0 copy-start
  2.1 0.1 copy.18
  2.2 0.5 copy-done.3
  2.8 0.1 copy.19
  2.9 0.0 copy-done.4
  2.9 0.1 copy.20.gain_in_ref
  3.0 0.0 copy-done.5
  3.0 0.1 copy.21.gain_out_ref
  3.2 0.0 copy-done.1
  3.2 0.2 copy.17
  3.4 0.0 copy-done
  3.4 180.9 %triangles.1 = bf16[8,256,128]{2,1,0:T(8,128)(2,1)S(1)} custom-call(bf16[8,256,128]{2,1,0:T(8,128)(2,1)S(1)} %copy-done, f32[2,8,1,128]{3,2,1,0:T(1,128)S(1)} %broadcast_multiply_fusion.mask_ref, f32[2,128,1]{2,1,0:T(8,128)S(1)} %copy.20.gain_in_ref, bf16[2,2,256,128]{3,2,1,0:T(8,128)(2,1)S(1)} %bitcast.11, bf16[2,128,128]{2,1,0:T(8,128)(2,1)S(1)} %bitcast.12, ...), custom_call_target="tpu_custom_call" | custom-call | tf_op jit(solution)/shard_map/triangles/pallas_call | solution.py:358
  184.3 0.8 copy.23
  (2 shorter events, 0.0 us)
Async XLA Ops:
  0.0 2.1 %copy-start.2 = (bf16[2,128,128]{2,1,0:T(8,128)(2,1)S(1)}, bf16[2,128,128]{2,1,0:T(8,128)(2,1)}, u32[]{:S(2)}) copy-start(bf16[2,128,128]{2,1,0:T(8,128)(2,1)} %param.13) | copy-start | bytes 196612
  1.8 1.1 copy-start.4
  1.9 0.8 copy-start.3
  2.0 1.0 copy-start.5
  2.0 1.2 copy-start.1
  2.1 1.3 copy-start

commit v4 on v3

--- a/solution.py
+++ b/solution.py
@@ -16,6 +16,7 @@
 GRP = 4
 GROUPS = 4
 SLOTS = DAP // GROUPS
+STEPS = Z // GROUPS
 ROWS, COLS, CHAN = 8, 256, 128
 BLOCK = SLOTS * ROWS
 HALF = COLS // 2
@@ -47,20 +48,30 @@
     both_sem, late_left_sem, late_right_sem, turned_sem,
 ):
     me, grp = lax.axis_index("dap"), lax.axis_index("grp")
-    z, plane = me % Z, me // Z
-
-    def spot(slot):
-        p = slot // PLANES
-        half = p // 2
-        return 8 + half - (p % 2) * (2 * half + 1), PLANES - 1 - slot % PLANES
-
-    def target(slot):
-        along, across = spot(slot)
-        return ((plane + across) % PLANES) * Z + (z + along) % Z
-
-    def origin(slot):
-        along, across = spot(slot)
-        return ((plane + PLANES - across) % PLANES) * Z + (z + Z - along) % Z
+    z, plane = lax.rem(me, Z), lax.div(me, Z)
+
+    planes_on = [lax.rem(plane + (PLANES - 1 - a), PLANES) * Z for a in range(PLANES)]
+    planes_back = [lax.rem(plane + (a + 1), PLANES) * Z for a in range(PLANES)]
+
+    def along(p):
+        half = lax.div(p, 2)
+        return 8 + half - lax.rem(p, 2) * (2 * half + 1)
+
+    def slots(lo, hi, body, back=False):
+        planes = planes_back if back else planes_on
+
+        def one(p, count):
+            there = lax.rem(z + Z - along(p), Z) if back else lax.rem(z + along(p), Z)
+            for a in range(count):
+                body(p * PLANES + a, planes[a] + there)
+
+        def step(p, carry):
+            one(p, PLANES)
+            return carry
+
+        lax.fori_loop(lo, min(hi, Z - 1), step, 0)
+        if hi == Z:
+            one(jnp.int32(Z - 1), PLANES - 1)
 
     def remote(src, dst, send, recv, dap=None, mate=None):
         device = {"dap": dap} if mate is None else {"grp": mate}
@@ -73,12 +84,12 @@
             device_id_type=MESH,
         )
 
-    def each(lo, hi, body):
+    def each(lo, hi, body, unroll=4):
         def step(i, carry):
             body(i)
             return carry
 
-        lax.fori_loop(lo, hi, step, 0)
+        lax.fori_loop(lo, hi, step, 0, unroll=unroll)
 
     def received(ref, sem):
         remote(ref, ref, 0, sem, dap=me).wait_recv()
@@ -91,12 +102,12 @@
 
     barrier = pltpu.get_barrier_semaphore()
 
-    def greet(slot):
-        pl.semaphore_signal(barrier, inc=1, device_id={"dap": target(slot)}, device_id_type=MESH)
-
-    each(0, DAP - 1, greet)
+    def greet(slot, other):
+        pl.semaphore_signal(barrier, inc=1, device_id={"dap": other}, device_id_type=MESH)
+
+    slots(0, Z, greet)
     for turn in range(1, GRP):
-        pl.semaphore_signal(barrier, inc=1, device_id={"grp": (grp + turn) % GRP}, device_id_type=MESH)
+        pl.semaphore_signal(barrier, inc=1, device_id={"grp": lax.rem(grp + turn, GRP)}, device_id_type=MESH)
 
     def turn_in(r):
         for s in range(2):
@@ -134,16 +145,15 @@
 
         each(0, ROWS, row)
 
-    def send_slots(src, got, send, sem_of, lo, hi):
-        def one(slot):
-            other = target(slot)
-            remote(src.at[other], got.at[slot], send, sem_of, dap=other).start()
-
-        each(lo, hi, one)
+    def send_slots(src, got, send, sem, lo, hi):
+        def one(slot, other):
+            remote(src.at[other], got.at[slot], send, sem, dap=other).start()
+
+        slots(lo, hi, one)
 
     def send_groups(src, got, send, sems, own):
         for k in range(GROUPS):
-            send_slots(src, got, send, sems.at[k], k * SLOTS, min((k + 1) * SLOTS, DAP - 1))
+            send_slots(src, got, send, sems.at[k], k * STEPS, (k + 1) * STEPS)
         own_copy(src.at[me], got.at[DAP - 1], own).start()
 
     def wait_group(src, got, sems, own, k):
@@ -175,11 +185,10 @@
     pack(right_src, 2 * ROWS)
     pl.semaphore_wait(barrier, DAP - 1 + GRP - 1)
 
-    def send_right(slot):
-        other = target(slot)
+    def send_right(slot, other):
         remote(right_src.at[other], right_got.at[me], 0, right_sem, dap=other).start()
 
-    each(0, DAP - 1, send_right)
+    slots(0, Z, send_right)
     own_copy(right_src.at[me], right_got.at[me], 0).start()
     for s in range(2):
         operand(0, 0, s, s * ROWS, 2 * ROWS)
@@ -202,7 +211,7 @@
     for q in range(GRP):
         unpack_wide(right_got, q * SLOTS, right_own.at[q])
     for turn in range(1, GRP):
-        mate = (grp + turn) % GRP
+        mate = lax.rem(grp + turn, GRP)
         remote(right_own.at[mate], right_mates.at[grp], 3, right_mate_sem, mate=mate).start()
     right_mates[grp] = right_own[grp]
 
@@ -210,7 +219,7 @@
         wait_group(left_src, left_got, left_sem, 1, k)
         unpack_wide(left_got, k * SLOTS, left_all.at[k, grp])
         for turn in range(1, GRP):
-            mate = (grp + turn) % GRP
+            mate = lax.rem(grp + turn, GRP)
             remote(left_all.at[k, grp], left_all.at[k, grp], 4, left_mate_sem.at[k], mate=mate).start()
 
     def rows_of(k):
@@ -225,10 +234,10 @@
             tri_src[0, s, pl.ds(k * SLOTS, SLOTS)] = part.astype(BF16)
 
     def return_rows(k, s):
-        def one(slot):
-            remote(tri_src.at[0, s, slot], tri_got.at[0, s, me], 2, tri_sem.at[0, s], dap=origin(slot)).start()
-
-        each(k * SLOTS, min((k + 1) * SLOTS, DAP - 1), one)
+        def one(slot, other):
+            remote(tri_src.at[0, s, slot], tri_got.at[0, s, me], 2, tri_sem.at[0, s], dap=other).start()
+
+        slots(k * STEPS, (k + 1) * STEPS, one, back=True)
 
     take_left(0)
     received(right_mates.at[pl.ds(0, GRP - 1)], right_mate_sem)
@@ -259,7 +268,7 @@
     send_groups(late_src.at[0], late_got.at[0], 6, late_left_sem, 4)
     operand(1, 1, 1, 0, ROWS)
     pack(late_src.at[1], ROWS)
-    send_slots(late_src.at[1], late_got.at[1], 7, late_right_sem, 0, DAP - 1)
+    send_slots(late_src.at[1], late_got.at[1], 7, late_right_sem, 0, Z)
     own_copy(late_src.at[1, me], late_got.at[1, DAP - 1], 5).start()
     for s in range(2):
         gates(1, s)
@@ -275,7 +284,7 @@
         at = pl.ds(k * BLOCK, BLOCK)
         left_t[s, grp, :, at] = unpacked[...].astype(F32).T.astype(BF16)
         for turn in range(1, GRP):
-            mate = (grp + turn) % GRP
+            mate = lax.rem(grp + turn, GRP)
             part = left_t.at[s, grp, :, at]
             remote(part, part, 8, turned_sem.at[s], mate=mate).start()
 
@@ -286,19 +295,25 @@
             tri_src[1, s, pl.ds(first, Z)] = value.reshape(Z, ROWS, HALF).astype(BF16)
 
     def return_quadrant(rows_half, s):
-        odd = (plane + rows_half) % 2
-
-        def one(i):
-            along, _ = spot((i // 4) * PLANES)
-            across = 2 * (3 - i % 4) + odd
-            other = ((plane + across) % PLANES) * Z + (z + along) % Z
+        odd = lax.rem(plane + rows_half, 2)
+        planes = [lax.rem(plane + (2 * a + odd), PLANES) * Z for a in (3, 2, 1, 0)]
+
+        def one(other):
             remote(tri_src.at[1, s, other], tri_got.at[1, s, me], 9, tri_sem.at[1, s], dap=other).start()
 
-        each(0, 4 * Z - 1, one)
+        def step(p, carry):
+            there = lax.rem(z + along(p), Z)
+            for first in planes:
+                one(first + there)
+            return carry
+
+        lax.fori_loop(0, Z - 1, step, 0)
+        for first in planes[:3]:
+            one(first + z)
 
         @pl.when(odd == 1)
         def _():
-            one(4 * Z - 1)
+            one(planes[3] + z)
 
     def keep_own(s):
         own_triangle = own_copy(tri_src.at[1, s, me], tri_got.at[1, s, me], 6)

time: 186 us -> 175 us (0.941)
  Pallas kernels: 181 us -> 171 us
    pallas_call x1, Pallas kernels: 181 us -> 171 us  [shards(): pl.pallas_call(kernel, out_shape=jax.ShapeDtypeStruct(pair_rep.shape, BF1...]
where the time goes in v4:
time: 175 us
  Pallas kernels  171 us (98%)
  local copies, waits for them, and re-layouts  2.19 us (1%)
  other arithmetic  1.89 us (1%)
    pallas_call x1, Pallas kernels, shards(): pl.pallas_call(kernel, out_shape=jax.ShapeDtypeStruct(pair_rep.shape, BF1...  171 us

profile of v4, /device:TPU:25, one launch (start us, length us, event | category | flops | bytes accessed | tf_op | source)
XLA Modules:
  0.0 174.8 jit_solution(5112372297699304126)
XLA Ops:
  0.0 0.0 copy-start.2
  0.0 0.8 convert_reduce_fusion
  0.8 0.2 reduce-window.8
  1.0 0.8 select_reduce_fusion.1
  1.8 0.0 copy-start.4
  1.8 0.1 dynamic_slice.6
  1.9 0.0 copy-start.3
  1.9 0.1 dynamic-slice_bitcast_fusion
  2.0 0.0 copy-start.5
  2.0 0.0 copy-start.1
  2.0 0.1 broadcast_multiply_fusion.mask_ref
  2.1 0.0 copy-done.2
  2.1 0.0 copy-start
  2.1 0.1 copy.18
  2.2 0.5 copy-done.3
  2.8 0.1 copy.19
  2.9 0.0 copy-done.4
  2.9 0.1 copy.20.gain_in_ref
  3.0 0.0 copy-done.5
  3.0 0.1 copy.21.gain_out_ref
  3.2 0.0 copy-done.1
  3.2 0.2 copy.17
  3.4 0.0 copy-done
  3.4 170.6 %triangles.1 = bf16[8,256,128]{2,1,0:T(8,128)(2,1)S(1)} custom-call(bf16[8,256,128]{2,1,0:T(8,128)(2,1)S(1)} %copy-done, f32[2,8,1,128]{3,2,1,0:T(1,128)S(1)} %broadcast_multiply_fusion.mask_ref, f32[2,128,1]{2,1,0:T(8,128)S(1)} %copy.20.gain_in_ref, bf16[2,2,256,128]{3,2,1,0:T(8,128)(2,1)S(1)} %bitcast.11, bf16[2,128,128]{2,1,0:T(8,128)(2,1)S(1)} %bitcast.12, ...), custom_call_target="tpu_custom_call" | custom-call | tf_op jit(solution)/shard_map/triangles/pallas_call | solution.py:373
  174.0 0.8 copy.23
  (2 shorter events, 0.0 us)
Async XLA Ops:
  0.0 2.1 %copy-start.2 = (bf16[2,128,128]{2,1,0:T(8,128)(2,1)S(1)}, bf16[2,128,128]{2,1,0:T(8,128)(2,1)}, u32[]{:S(2)}) copy-start(bf16[2,128,128]{2,1,0:T(8,128)(2,1)} %param.13) | copy-start | bytes 196612
  1.8 1.1 copy-start.4
  1.9 0.8 copy-start.3
  2.0 1.0 copy-start.5
  2.0 1.2 copy-start.1
  2.1 1.3 copy-start

commit v5 on v4

--- a/solution.py
+++ b/solution.py
@@ -22,29 +22,19 @@
 HALF = COLS // 2
 
 
-def residue_valid(chain_ids, crop_lengths):
-    count = chain_ids.shape[0]
-    chains = jnp.arange(crop_lengths.shape[0], dtype=jnp.int32)
-    member = (chain_ids[:, None] == chains[None, :]).astype(jnp.int32)
-    counts = jnp.sum(member, axis=0)
-    starts = jnp.cumsum(counts) - counts
-    first = jnp.sum(member * starts[None, :], axis=1)
-    limit = jnp.sum(member * crop_lengths[None, :], axis=1)
-    place = jnp.arange(count, dtype=jnp.int32) - first
-    return (place < limit).astype(jnp.float32)
-
-
 def sigmoid(v):
     return 0.5 * jnp.tanh(0.5 * v) + 0.5
 
 
 def kernel(
-    pair_ref, mask_ref, gain_in_ref, w_proj_ref, w_gate_ref, gain_out_ref, w_out_ref,
+    pair_hbm, chain_hbm, crop_ref, ln_in_hbm, w_proj_hbm, w_gate_hbm, ln_out_hbm, w_out_hbm,
     out_ref,
+    pair_ref, chain_ref, ln_in_ref, w_proj_ref, w_gate_ref, ln_out_ref, w_out_ref,
+    kept_ref, mask_ref, gain_in, gain_out, w_proj_t, w_gate_t, w_out_t,
     pair_t, normed, gate, staged, product,
     right_src, left_src, right_got, left_got, right_own, right_mates, left_all, tri_src, tri_got,
     both_src, both_got, late_src, late_got, unpacked, left_t, right_m,
-    own_sem, send_sem, right_sem, left_sem, right_mate_sem, left_mate_sem, tri_sem,
+    in_sem, own_sem, send_sem, right_sem, left_sem, right_mate_sem, left_mate_sem, tri_sem,
     both_sem, late_left_sem, late_right_sem, turned_sem,
 ):
     me, grp = lax.axis_index("dap"), lax.axis_index("grp")
@@ -84,7 +74,7 @@
             device_id_type=MESH,
         )
 
-    def each(lo, hi, body, unroll=4):
+    def each(lo, hi, body, unroll=8):
         def step(i, carry):
             body(i)
             return carry
@@ -100,6 +90,22 @@
     def own_copy(src, dst, sem):
         return pltpu.make_async_copy(src, dst, own_sem.at[sem])
 
+    inputs = [
+        pltpu.make_async_copy(src, dst, in_sem.at[i])
+        for i, (src, dst) in enumerate(
+            [
+                (pair_hbm, pair_ref),
+                (chain_hbm, chain_ref),
+                (ln_in_hbm, ln_in_ref),
+                (w_proj_hbm, w_proj_ref),
+                (w_gate_hbm, w_gate_ref),
+                (ln_out_hbm, ln_out_ref),
+                (w_out_hbm, w_out_ref),
+            ]
+        )
+    ]
+    for copy in inputs:
+        copy.start()
     barrier = pltpu.get_barrier_semaphore()
 
     def greet(slot, other):
@@ -109,10 +115,45 @@
     for turn in range(1, GRP):
         pl.semaphore_signal(barrier, inc=1, device_id={"grp": lax.rem(grp + turn, GRP)}, device_id_type=MESH)
 
+    def turned(block):
+        return block.astype(F32).T.astype(BF16)
+
+    def turn_projection(u, which):
+        for part in range(2):
+            at = (2 * which + part) * CHAN
+            w_proj_t[u, which, part * CHAN : (part + 1) * CHAN] = turned(w_proj_ref[u, :, at : at + CHAN])
+
+    def turn_gain(u):
+        gain_in[u] = jnp.broadcast_to(ln_in_ref[u : u + 1], (CHAN, CHAN)).T
+        gain_out[u] = jnp.broadcast_to(ln_out_ref[u : u + 1], (CHAN, CHAN)).T
+
+    def residue_mask():
+        ids = chain_ref[...]
+        sublane = lax.broadcasted_iota(jnp.int32, (8, 128), 0)
+        lane = lax.broadcasted_iota(jnp.int32, (8, 128), 1)
+        place = (sublane * 128 + lane).astype(F32)
+        start, first, limit = jnp.zeros((1, 1), F32), jnp.zeros((8, 128), F32), jnp.zeros((8, 128), F32)
+        for chain in range(crop_ref.shape[0]):
+            member = (ids == chain).astype(F32)
+            first += member * start
+            limit += member * crop_ref[chain].astype(F32)
+            start += jnp.sum(jnp.sum(member, axis=1, keepdims=True), axis=0, keepdims=True)
+        kept = (place - first < limit).astype(F32)
+        for i in range(8):
+            kept_ref[i] = kept[i : i + 1]
+        mine = lane == sublane + lax.rem(me, Z) * ROWS
+        kept_rows = jnp.sum(jnp.where(mine, kept_ref[plane], 0.0), axis=1, keepdims=True)
+        for s in range(2):
+            mask = kept_rows * kept_ref[2 * grp + s]
+            for r in range(ROWS):
+                mask_ref[s, r] = mask[r : r + 1]
+
     def turn_in(r):
         for s in range(2):
-            pair_t[s, r] = pair_ref[r, s * HALF : (s + 1) * HALF].astype(F32).T.astype(BF16)
-
+            pair_t[s, r] = turned(pair_ref[r, s * HALF : (s + 1) * HALF])
+
+    for copy in inputs:
+        copy.wait()
     each(0, ROWS, turn_in)
 
     def normalise(u, s):
@@ -120,15 +161,26 @@
             x = pair_t[s, r].astype(F32)
             centred = x - jnp.mean(x, axis=0, keepdims=True)
             spread = jnp.mean(centred * centred, axis=0, keepdims=True)
-            normed[s, r] = (centred * lax.rsqrt(spread + epsilon_norm) * gain_in_ref[u]).astype(BF16)
+            normed[s, r] = (centred * lax.rsqrt(spread + epsilon_norm) * gain_in[u]).astype(BF16)
 
         each(0, ROWS, row)
 
     def operand(u, which, s, first, stride):
         def row(r):
-            both = jnp.dot(w_proj_ref[u, which], normed[s, r], preferred_element_type=F32)
+            both = jnp.dot(w_proj_t[u, which], normed[s, r], preferred_element_type=F32)
             value = sigmoid(both[:CHAN]) * both[CHAN:] * mask_ref[s, r]
             staged[pl.ds(first + r, CHAN, stride=stride), :] = value
+
+        each(0, ROWS, row)
+
+    def operand_wide(which):
+        def row(r):
+            wide = jnp.concatenate([normed[0, r], normed[1, r]], axis=1)
+            both = jnp.dot(w_proj_t[0, which], wide, preferred_element_type=F32)
+            value = sigmoid(both[:CHAN]) * both[CHAN:]
+            for s in range(2):
+                half = value[:, s * HALF : (s + 1) * HALF] * mask_ref[s, r]
+                staged[pl.ds(s * ROWS + r, CHAN, stride=2 * ROWS), :] = half
 
         each(0, ROWS, row)
 
@@ -141,7 +193,7 @@
 
     def gates(u, s):
         def row(r):
-            gate[s, r] = sigmoid(jnp.dot(w_gate_ref[u], normed[s, r], preferred_element_type=F32))
+            gate[s, r] = sigmoid(jnp.dot(w_gate_t[u], normed[s, r], preferred_element_type=F32))
 
         each(0, ROWS, row)
 
@@ -166,11 +218,11 @@
         x = tri_got[u, s].astype(F32)
         centred = x - jnp.mean(x, axis=0, keepdims=True)
         spread = jnp.mean(centred * centred, axis=0, keepdims=True)
-        product[...] = (centred * lax.rsqrt(spread + epsilon_norm)).reshape(CHAN * ROWS, 128)
+        product[pl.ds(0, CHAN * ROWS), :] = (centred * lax.rsqrt(spread + epsilon_norm)).reshape(CHAN * ROWS, 128)
 
         def row(r):
-            scaled = (product[pl.ds(r, CHAN, stride=ROWS), :] * gain_out_ref[u]).astype(BF16)
-            term = jnp.dot(w_out_ref[u], scaled, preferred_element_type=F32)
+            scaled = (product[pl.ds(r, CHAN, stride=ROWS), :] * gain_out[u]).astype(BF16)
+            term = jnp.dot(w_out_t[u], scaled, preferred_element_type=F32)
             result = pair_t[s, r].astype(F32) + gate[s, r] * term
             if last:
                 out_ref[r, s * HALF : (s + 1) * HALF] = result.T.astype(BF16)
@@ -179,9 +231,12 @@
 
         each(0, ROWS, row)
 
+    residue_mask()
+    turn_gain(0)
+    turn_projection(0, 1)
     for s in range(2):
         normalise(0, s)
-        operand(0, 1, s, s * ROWS, 2 * ROWS)
+    operand_wide(1)
     pack(right_src, 2 * ROWS)
     pl.semaphore_wait(barrier, DAP - 1 + GRP - 1)
 
@@ -190,12 +245,18 @@
 
     slots(0, Z, send_right)
     own_copy(right_src.at[me], right_got.at[me], 0).start()
-    for s in range(2):
-        operand(0, 0, s, s * ROWS, 2 * ROWS)
+    turn_projection(0, 0)
+    operand_wide(0)
     pack(left_src, 2 * ROWS)
     send_groups(left_src, left_got, 1, left_sem, 1)
+    for u in range(2):
+        w_gate_t[u] = turned(w_gate_ref[u])
+        w_out_t[u] = turned(w_out_ref[u])
     for s in range(2):
         gates(0, s)
+    turn_gain(1)
+    for which in range(2):
+        turn_projection(1, which)
 
     def unpack_wide(got, first, dst):
         def some(i):
@@ -360,27 +421,36 @@
 
 
 def shards(pair_rep, chain_ids, crop_lengths, ln_in_gain, w_proj, w_gate, ln_out_gain, w_out):
-    kept = residue_valid(chain_ids, crop_lengths)
-    kept_rows = lax.dynamic_slice_in_dim(kept, lax.axis_index("dap") * ROWS, ROWS, 0)
-    kept_columns = lax.dynamic_slice_in_dim(kept, lax.axis_index("grp") * COLS, COLS, 0)
-    pair_mask = kept_rows[None, :, None, None] * kept_columns.reshape(2, 1, 1, HALF)
-    w_proj_t = w_proj.transpose(0, 2, 1).reshape(2, 2, 2 * CHAN, CHAN)
+    hbm = pl.BlockSpec(memory_space=pltpu.HBM)
     vmem = pl.BlockSpec(memory_space=pltpu.VMEM)
+    chain_tile = chain_ids.reshape(8, 128)
     wide, narrow = (DAP, 2 * ROWS, 128), (DAP, ROWS, 128)
     turned = (2, ROWS, CHAN, HALF)
+    weight = (2, CHAN, CHAN)
     square = (BLOCK, COLS)
     dma = pltpu.SemaphoreType.DMA
     return pl.pallas_call(
         kernel,
         out_shape=jax.ShapeDtypeStruct(pair_rep.shape, BF16),
-        in_specs=[vmem] * 7,
+        in_specs=[hbm, hbm, pl.BlockSpec(memory_space=pltpu.SMEM)] + [hbm] * 5,
         out_specs=vmem,
         scratch_shapes=[
+            *(
+                pltpu.VMEM(x.shape, x.dtype)
+                for x in (pair_rep, chain_tile, ln_in_gain, w_proj, w_gate, ln_out_gain, w_out)
+            ),
+            pltpu.VMEM((8, 1, 128), F32),
+            pltpu.VMEM((2, ROWS, 1, HALF), F32),
+            pltpu.VMEM(weight, F32),
+            pltpu.VMEM(weight, F32),
+            pltpu.VMEM((2, 2, 2 * CHAN, CHAN), BF16),
+            pltpu.VMEM(weight, BF16),
+            pltpu.VMEM(weight, BF16),
             pltpu.VMEM(turned, BF16),
             pltpu.VMEM(turned, BF16),
             pltpu.VMEM(turned, F32),
-            pltpu.VMEM((CHAN * 2 * ROWS, 128), F32),
-            pltpu.VMEM((CHAN * ROWS, 128), F32),
+            pltpu.VMEM((CHAN * 2 * ROWS + 2 * ROWS, 128), F32),
+            pltpu.VMEM((CHAN * ROWS + ROWS, 128), F32),
             pltpu.VMEM(wide, BF16),
             pltpu.VMEM(wide, BF16),
             pltpu.VMEM(wide, BF16),
@@ -397,6 +467,7 @@
             pltpu.VMEM((BLOCK, HALF), BF16),
             pltpu.VMEM((2, GRP, HALF, DAP * ROWS), BF16),
             pltpu.VMEM((2, DAP * ROWS, HALF), BF16),
+            dma((7,)),
             dma((7,)),
             dma((10,)),
             dma,
@@ -410,18 +481,10 @@
             dma((2,)),
         ],
         compiler_params=pltpu.CompilerParams(
-            collective_id=0, has_side_effects=True, vmem_limit_bytes=40 << 20
+            collective_id=0, has_side_effects=True, vmem_limit_bytes=63 << 20
         ),
         name="triangles",
-    )(
-        pair_rep,
-        pair_mask,
-        ln_in_gain[:, :, None],
-        w_proj_t,
-        w_gate.transpose(0, 2, 1),
-        ln_out_gain[:, :, None],
-        w_out.transpose(0, 2, 1),
-    )
+    )(pair_rep, chain_tile, crop_lengths, ln_in_gain, w_proj, w_gate, ln_out_gain, w_out)
 
 
 def solution(mesh):

time: 175 us -> 174 us (level)
  other arithmetic: 1.89 us -> 0 us
where the time goes in v5:
time: 174 us
  Pallas kernels  172 us (99%)
  local copies, waits for them, and re-layouts  1.87 us (1%)
    pallas_call x1, Pallas kernels, shards(): pl.pallas_call(kernel, out_shape=jax.ShapeDtypeStruct(pair_rep.shape, BF1...  172 us

profile of v5, /device:TPU:25, one launch (start us, length us, event | category | flops | bytes accessed | tf_op | source)
XLA Modules:
  0.0 173.6 jit_solution(10881766805754938702)
XLA Ops:
  0.0 171.8 %triangles.1 = bf16[8,256,128]{2,1,0:T(8,128)(2,1)} custom-call(bf16[8,256,128]{2,1,0:T(8,128)(2,1)} %pair_hbm.1, s32[8,128]{1,0:T(8,128)} %bitcast.1, s32[8]{0:T(128)} %crop_ref.1, f32[2,128]{1,0:T(2,128)} %ln_in_hbm.1, bf16[2,128,512]{2,1,0:T(8,128)(2,1)} %w_proj_hbm.1, bf16[2,128,128]{2,1,0:T(8,128)(2,1)} %w_gate_hbm.1, f32[2,128]{1,0:T(2,128)} %ln_out_hbm.1, ...), custom_call_target="tpu_custom_call" | custom-call | tf_op jit(solution)/shard_map/triangles/pallas_call | solution.py:432
  171.8 1.9 %copy.10 = bf16[8,256,128]{2,1,0:T(8,128)(2,1)} copy(bf16[8,256,128]{2,1,0:T(8,128)(2,1)} %triangles.1) | data formatting | bytes 1048576
